TPU v7x, 256 devices: a whole 4x4x8 slice. The times are simulated.
256 devices in a mesh: req: 16 (over y, x_hi, core), tp: 16 (over x_lo, z).
Axes of the slice: x: 4 (x_hi: 2, x_lo: 2; x = x_hi * 2 + x_lo), y: 4, z: 8, core: 2. Of those that a mesh axis runs over, the one named last changes fastest.
Arguments:
- patches: bfloat16 [16, 1024, 1664], P('req', 'tp'), may hold values from -6 to 6
- vis_gain: float32 [1664], replicated, may hold values from 0.1 to 1.9
- w_fc1: bfloat16 [1664, 8192], P(None, 'tp'), may hold values from -0.15625 to 0.15625
- w_fc2: bfloat16 [8192, 1664], P('tp'), may hold values from -0.125 to 0.125
- merge_gain: float32 [1664], replicated, may hold values from 0.1 to 1.9
- w_merge: bfloat16 [6656, 1664], P('tp'), may hold values from -0.078125 to 0.078125
- slots: int32 [16, 256], P('req'), may hold values from 0 to 3071, as said below
- text: bfloat16 [16, 3072, 1664], P('req', 'tp'), may hold values from -6 to 6
- docs: int32 [16, 3072], P('req'), may hold values from 0 to 7, never falling along the last dimension, each value on 1 to 768 neighbouring positions
- dec_gain: float32 [1664], replicated, may hold values from 0.1 to 1.9
- w_qkv: bfloat16 [1664, 4992], P(None, 'tp'), may hold values from -0.2773501 to 0.2773501
- w_out: bfloat16 [1664, 1664], P('tp'), may hold values from -0.625 to 0.625
Outputs:
- decoded: bfloat16 [16, 3072, 1664], P('req', 'tp')
Inputs may be any that keep to these rules, and one draw needn't show every extreme that they name: `slots`: positions in a group are distinct; each image's 64 merged rows take consecutive positions in order, and image k lies within positions j * 768 to (j + 1) * 768 - 1 with j = (k + 2) mod 4; the image with j = 3 takes the last 64 positions of the prompt. `docs`: request numbers never fall along a prompt; each request spans 1 to 768 positions.
All inputs are finite; a program needn't handle non-finite values.
Results may differ from a plain program's by a relative error of at most 0.033.
Values may be sent and summed in bfloat16 or wider, within the bound.
A program may use at most 64 MiB of HBM per device.

v0:
```python
import math

import jax
import jax.numpy as jnp
from jax import lax
from jax.sharding import PartitionSpec as P

HD = 104


EPSILON = 1e-06


def layer_norm(values, gains):
    average = jnp.mean(values, axis=-1, keepdims=True)
    centred = values - average
    variance = jnp.mean(centred * centred, axis=-1, keepdims=True)
    return centred * lax.rsqrt(variance + EPSILON) * gains


def rms_norm(values, gains):
    return values * lax.rsqrt(jnp.mean(values * values, axis=-1, keepdims=True) + EPSILON) * gains


def attend(qkv_rows, doc_row, heads_here):
    seq_len = qkv_rows.shape[0]
    block_rows = min(512, seq_len)
    shaped = qkv_rows.reshape(seq_len, heads_here, 3, HD)
    queries = shaped[:, :, 0]
    key_rows = shaped[:, :, 1]
    value_rows = shaped[:, :, 2]
    key_pos = jnp.arange(seq_len)

    def one_block(block_index):
        offset = block_index * block_rows
        query_block = lax.dynamic_slice_in_dim(queries, offset, block_rows, 0)
        query_pos = offset + jnp.arange(block_rows)
        query_docs = lax.dynamic_slice_in_dim(doc_row, offset, block_rows, 0)
        scores = jnp.einsum(
            "qhe,khe->hqk", query_block, key_rows, preferred_element_type=jnp.float32
        ) / math.sqrt(HD)
        allowed = (key_pos[None, :] <= query_pos[:, None]) & (
            doc_row[None, :] == query_docs[:, None]
        )
        scores = jnp.where(allowed[None], scores, -1e30)
        largest = jnp.max(scores, axis=-1, keepdims=True)
        raised = jnp.where(allowed[None], jnp.exp(scores - largest), 0.0)
        weights = (raised / jnp.sum(raised, axis=-1, keepdims=True)).astype(jnp.bfloat16)
        blended = jnp.einsum(
            "hqk,khe->qhe", weights, value_rows, preferred_element_type=jnp.float32
        )
        return blended.astype(jnp.bfloat16).reshape(block_rows, heads_here * HD)

    blocks = lax.map(one_block, jnp.arange(seq_len // block_rows))
    return blocks.reshape(seq_len, heads_here * HD)


def shards(
    patches, vis_gain, w_fc1, w_fc2, merge_gain, w_merge, slots, text, docs, dec_gain, w_qkv, w_out
):
    patch_rows = patches[0]
    slot_row = slots[0]
    text_rows = text[0]
    doc_row = docs[0]
    width = patch_rows.shape[1]
    local_rows = patch_rows.shape[0]
    seq_here = text_rows.shape[0]
    wide_in = patch_rows.astype(jnp.float32)
    normed_in = layer_norm(wide_in, vis_gain).astype(jnp.bfloat16)
    hidden = jax.nn.gelu(
        jnp.dot(
            lax.all_gather(normed_in, "tp", axis=0, tiled=True),
            w_fc1,
            preferred_element_type=jnp.float32,
        ),
        approximate=False,
    ).astype(jnp.bfloat16)
    mlp_sum = lax.psum_scatter(
        jnp.dot(hidden, w_fc2, preferred_element_type=jnp.float32).astype(jnp.bfloat16),
        "tp",
        scatter_dimension=0,
        tiled=True,
    ).astype(jnp.float32)
    normed_out = layer_norm(wide_in + mlp_sum, merge_gain).astype(jnp.bfloat16)
    merge_in = normed_out.reshape(local_rows // 4, 4 * width)
    features = lax.all_to_all(merge_in, "tp", split_axis=1, concat_axis=0, tiled=True)
    merge_term = jnp.dot(features, w_merge, preferred_element_type=jnp.float32)
    merged_share = lax.psum_scatter(
        merge_term.astype(jnp.bfloat16), "tp", scatter_dimension=0, tiled=True
    )
    merged = lax.all_gather(merged_share, "tp", axis=0, tiled=True)
    positions = lax.axis_index("tp") * seq_here + jnp.arange(seq_here, dtype=jnp.int32)
    matches = slot_row[None, :] == positions[:, None]
    placed = jnp.dot(
        matches.astype(jnp.bfloat16), merged, preferred_element_type=jnp.float32
    ).astype(jnp.bfloat16)
    embedded = jnp.where(jnp.any(matches, axis=1)[:, None], placed, text_rows)
    dec_in = rms_norm(embedded.astype(jnp.float32), dec_gain).astype(jnp.bfloat16)
    qkv_rows = jnp.dot(
        lax.all_gather(dec_in, "tp", axis=0, tiled=True), w_qkv, preferred_element_type=jnp.float32
    ).astype(jnp.bfloat16)
    heads_here = qkv_rows.shape[1] // (3 * HD)
    attended = attend(qkv_rows, doc_row, heads_here)
    out_sum = lax.psum_scatter(
        jnp.dot(attended, w_out, preferred_element_type=jnp.float32).astype(jnp.bfloat16),
        "tp",
        scatter_dimension=0,
        tiled=True,
    ).astype(jnp.float32)
    decoded = (embedded.astype(jnp.float32) + out_sum).astype(jnp.bfloat16)
    return decoded[None]


def solution(mesh):
    placed = (
        P("req", "tp", None),
        P(),
        P(None, "tp"),
        P("tp", None),
        P(),
        P("tp", None),
        P("req", None),
        P("req", "tp", None),
        P("req", None),
        P(),
        P(None, "tp"),
        P("tp", None),
    )
    return jax.shard_map(
        shards, mesh=mesh, in_specs=placed, out_specs=P("req", "tp", None), check_vma=False
    )
```

profile of v0, /device:TPU:1, one launch (start us, length us, event | category | flops | bytes accessed | tf_op | source)
XLA Modules:
  0.0 623.6 jit_solution(15786397968516002857)
XLA Ops:
  6.5 1.2 convert_reduce_fusion
  7.7 1.2 fusion.66
  8.9 1.8 fusion.68
  10.7 0.0 all-gather.3.cloned.1.call-update
  10.7 0.0 reduce-scatter.4.cloned.1.call-start
  10.8 70.4 %all-gather.3.cloned.1.call-done = bf16[1024,1664]{1,0:T(8,128)(2,1)} async-done(((bf16[64,1664]{1,0:T(8,128)(2,1)}), bf16[1024,1664]{1,0:T(8,128)(2,1)}) %all-gather.3.cloned.1.call-update) | async-done | bytes 3407888 | tf_op jit(solution)/shard_map/all_gather | solution.py:72
  81.1 11.6 %convolution_convert_fusion.2 = bf16[1024,1664]{1,0:T(8,128)(2,1)} fusion(bf16[512,1664]{1,0:T(8,128)(2,1)S(1)} %copy-done, bf16[1024,1664]{1,0:T(8,128)(2,1)} %all-gather.3.cloned.1.call-done, bf16[1664,512]{1,0:T(8,128)(2,1)} %param.16), kind=kOutput, calls=%fused_computation.24 | convolution fusion | flops 3525443584 | bytes 10223616 | tf_op jit(solution)/shard_map/dot_general | solution.py:79
  92.7 0.0 reduce-scatter.4.cloned.1.call-update
  92.7 0.0 reduce-scatter.6.cloned.1.call-start
  92.8 75.1 %reduce-scatter.4.cloned.1.call-done = bf16[64,1664]{1,0:T(8,128)(2,1)} async-done(((bf16[1024,1664]{1,0:T(8,128)(2,1)}), bf16[64,1664]{1,0:T(8,128)(2,1)}) %reduce-scatter.4.cloned.1.call-update) | async-done | bytes 213008 | tf_op jit(solution)/shard_map/reduce_scatter | solution.py:78
  167.9 1.1 fusion.70
  169.0 1.2 multiply_reduce_fusion.1
  170.2 1.1 multiply_convert_fusion.1
  171.3 0.3 all_to_all.14
  171.6 0.2 copy.18
  171.7 10.4 %all_to_all.19 = bf16[16,16,416]{2,0,1:T(8,128)(2,1)S(1)} all-to-all(bf16[16,16,416]{2,0,1:T(8,128)(2,1)S(1)} %copy.18), channel_id=1, replica_groups=mesh['req'=16,'tp'=16] {'tp'}, dimensions={1} | all-to-all | bytes 425984 | tf_op jit(solution)/shard_map/all_to_all | solution.py:86
  182.1 2.9 convolution_convert_fusion.3
  185.0 0.0 reduce-scatter.6.cloned.1.call-update
  185.0 0.0 all-gather.5.cloned.1.call-start
  185.1 0.2 compare_reduce_fusion
  185.3 68.8 %reduce-scatter.6.cloned.1.call-done = bf16[16,1664]{1,0:T(8,128)(2,1)} async-done(((bf16[256,1664]{1,0:T(8,128)(2,1)}), bf16[16,1664]{1,0:T(8,128)(2,1)}) %reduce-scatter.6.cloned.1.call-update) | async-done | bytes 53264 | tf_op jit(solution)/shard_map/reduce_scatter | solution.py:88
  254.1 30.6 %all_gather.10 = bf16[256,1664]{1,0:T(8,128)(2,1)S(1)} all-gather(bf16[16,1664]{1,0:T(8,128)(2,1)} %reduce-scatter.6.cloned.1.call-done), channel_id=1, replica_groups=mesh['req'=16,'tp'=16] {'tp'}, dimensions={0}, use_global_device_ids=true | all-gather | bytes 905216 | tf_op jit(solution)/shard_map/all_gather | solution.py:91
  284.7 1.6 multiply_reduce_fusion
  286.3 1.0 multiply_convert_fusion
  287.4 0.0 all-gather.5.cloned.1.call-update
  287.4 0.2 reduce-scatter.8.cloned.1.call-start
  287.6 132.2 %all-gather.5.cloned.1.call-done = bf16[3072,1664]{1,0:T(8,128)(2,1)} async-done(((bf16[192,1664]{1,0:T(8,128)(2,1)}), bf16[3072,1664]{1,0:T(8,128)(2,1)}) %all-gather.5.cloned.1.call-update) | async-done | bytes 10223632 | tf_op jit(solution)/shard_map/all_gather | solution.py:100
  419.8 7.8 %convolution_convert_fusion.1 = bf16[3072,312]{0,1:T(8,128)(2,1)S(1)} fusion(bf16[3072,1664]{1,0:T(8,128)(2,1)} %all-gather.5.cloned.1.call-done, bf16[1664,312]{0,1:T(8,128)(2,1)} %param.24), kind=kOutput, calls=%fused_computation.23 | convolution fusion | flops 3190726656 | bytes 13178880 | tf_op jit(solution)/shard_map/dot_general | solution.py:99
  427.6 1.3 slice_bitcast_fusion
  428.9 61.9 %while.11 = (s32[]{:T(128)}, bf16[6,512,104]{1,2,0:T(8,128)(2,1)}, s32[6]{0:T(128)S(1)}, s32[1,3072]{1,0:T(1,128)S(1)}, s32[3072]{0:T(1024)S(1)}, /*index=5*/bf1...) while((s32[]{:T(128)}, bf16[6,512,104]{1,2,0:T(8,128)(2,1)}, ...), condition=%wide.region_11.12_spmd.clone, body=%wide.region_8.11_spmd.clone.sunk | while | flops 690540032 | bytes 22987480 | solution.py:54
  428.9 0.5 dynamic_slice.23
  430.0 0.1 dynamic_slice.24
  430.1 3.2 fusion.121
  433.3 2.5 fusion.122
  435.8 3.4 fusion.123
  439.2 0.5 dynamic_slice.23
  440.4 0.1 dynamic_slice.24
  440.4 3.2 fusion.121
  443.6 2.5 fusion.122
  446.2 3.4 fusion.123
  449.6 0.5 dynamic_slice.23
  450.7 0.1 dynamic_slice.24
  450.8 3.2 fusion.121
  453.9 2.5 fusion.122
  456.5 3.4 fusion.123
  459.9 0.5 dynamic_slice.23
  461.0 0.1 dynamic_slice.24
  461.1 3.2 fusion.121
  464.3 2.5 fusion.122
  466.8 3.4 fusion.123
  470.2 0.5 dynamic_slice.23
  471.3 0.1 dynamic_slice.24
  471.4 3.2 fusion.121
  474.6 2.5 fusion.122
  477.1 3.4 fusion.123
  480.5 0.5 dynamic_slice.23
  481.6 0.1 dynamic_slice.24
  481.7 3.2 fusion.121
  484.9 2.5 fusion.122
  487.5 3.4 fusion.123
  490.9 1.1 copy.20
  492.0 5.4 convolution_convert_fusion
  497.5 117.6 %reduce-scatter.8.cloned.1.call-done = bf16[192,1664]{1,0:T(8,128)(2,1)} async-done(((bf16[3072,1664]{1,0:T(8,128)(2,1)}), bf16[192,1664]{1,0:T(8,128)(2,1)}) %reduce-scatter.8.cloned.1.call-update) | async-done | bytes 638992 | tf_op jit(solution)/shard_map/reduce_scatter | solution.py:104
  615.0 2.0 fusion.61
  (42 shorter events, 0.1 us)
Async XLA Ops:
  6.5 74.6 %copy-start = (bf16[512,1664]{1,0:T(8,128)(2,1)S(1)}, bf16[512,1664]{1,0:T(8,128)(2,1)}, u32[]{:S(2)}) copy-start(bf16[512,1664]{1,0:T(8,128)(2,1)} %param.17) | copy-start | bytes 5111812
  6.5 74.6 %all-gather.3.cloned.1.call-start = ((), (), s32[]{:S(2)}) async-start(), calls=%async_computation.4 | async-start | bytes 3620864 | tf_op jit(solution)/shard_map/all_gather | solution.py:72
  10.7 157.2 %reduce-scatter.4.cloned.1.call-start = ((), (), s32[]{:S(2)}) async-start(), calls=%async_computation.5 | async-start | bytes 3620864 | tf_op jit(solution)/shard_map/reduce_scatter | solution.py:78
  92.7 75.2 %copy-start.1 = (bf16[1,64,1664]{2,1,0:T(8,128)(2,1)S(1)}, bf16[1,64,1664]{2,1,0:T(8,128)(2,1)}, u32[]{:S(2)}) copy-start(bf16[1,64,1664]{2,1,0:T(8,128)(2,1)} %param.14) | copy-start | bytes 638980
  92.7 77.5 %copy-start.5 = (f32[1664]{0:T(1024)S(1)}, f32[1664]{0:T(1024)}, u32[]{:S(2)}) copy-start(f32[1664]{0:T(1024)} %param.18) | copy-start | bytes 19972
  92.7 161.4 %reduce-scatter.6.cloned.1.call-start = ((), (), s32[]{:S(2)}) async-start(), calls=%async_computation.6 | async-start | bytes 905216 | tf_op jit(solution)/shard_map/reduce_scatter | solution.py:88
  171.6 13.5 %copy-start.7 = (s32[1,256]{1,0:T(1,128)S(1)}, s32[1,256]{1,0:T(1,128)}, u32[]{:S(2)}) copy-start(s32[1,256]{1,0:T(1,128)} %param.20) | copy-start | bytes 3076
  185.0 101.3 %copy-start.6 = (f32[1664]{0:T(1024)S(1)}, f32[1664]{0:T(1024)}, u32[]{:S(2)}) copy-start(f32[1664]{0:T(1024)} %param.23) | copy-start | bytes 19972
  185.0 234.8 %all-gather.5.cloned.1.call-start = ((), (), s32[]{:S(2)}) async-start(), calls=%async_computation.7 | async-start | bytes 10862592 | tf_op jit(solution)/shard_map/all_gather | solution.py:100
  287.4 327.7 %reduce-scatter.8.cloned.1.call-start = ((), (), s32[]{:S(2)}) async-start(), calls=%async_computation.8 | async-start | bytes 10862592 | tf_op jit(solution)/shard_map/reduce_scatter | solution.py:104
  427.6 1.3 copy-start.3
  428.9 63.1 %copy-start.4 = (bf16[104,1664]{1,0:T(8,128)(2,1)S(1)}, bf16[104,1664]{1,0:T(8,128)(2,1)}, u32[]{:S(2)}) copy-start(bf16[104,1664]{1,0:T(8,128)(2,1)} %param.25) | copy-start | bytes 1038340
  433.3 2.5 copy-start.2
  443.6 2.5 copy-start.2
  453.9 2.5 copy-start.2
  464.3 2.5 copy-start.2
  474.6 2.5 copy-start.2
  484.9 2.5 copy-start.2
Sparse Core Ops, SparseCore 0:
  10.8 70.2 all-gather.2
  92.9 75.0 reduce-scatter.3
  185.1 68.9 reduce-scatter.5
  287.5 132.2 all-gather.4
  497.6 117.3 reduce-scatter.7
where the time goes:
time: 624 us
  waiting for transfers between devices  464 us (74%)
  matrix products  68.8 us (11%)
  blocking collectives  41 us (7%)
  other arithmetic  25.9 us (4%)
  between operations  13.3 us (2%)
  local copies, waits for them, and re-layouts  6.75 us (1%)
    all_gather x1, waiting for transfers between devices, shards(): lax.all_gather(dec_in, 'tp', axis=0, tiled=True)  132 us
    reduce_scatter x1, waiting for transfers between devices, shards(): lax.psum_scatter(jnp.dot(attended, w_out, preferred_element_type=jnp.floa...  118 us
    reduce_scatter x1, waiting for transfers between devices, shards(): lax.psum_scatter(jnp.dot(hidden, w_fc2, preferred_element_type=jnp.float3...  75.1 us
    all_gather x1, waiting for transfers between devices, shards(): lax.all_gather(normed_in, 'tp', axis=0, tiled=True)  70.4 us
    reduce_scatter x1, waiting for transfers between devices, shards(): lax.psum_scatter(merge_term.astype(jnp.bfloat16), 'tp', scatter_dimension...  68.8 us
    all_gather x1, blocking collectives, shards(): merged = lax.all_gather(merged_share, 'tp', axis=0, tiled=True)  30.6 us
    dot_general x6, matrix products, one_block(): jnp.einsum('hqk,khe->qhe', weights, value_rows, preferred_element_type=jn...  20.5 us
    dot_general x6, matrix products, one_block(): jnp.einsum('qhe,khe->hqk', query_block, key_rows, preferred_element_type=...  19 us
  transfers between devices with their start and end apart: 5, of which 5 were waited for; matrix products, arithmetic and copies ran while one was open for 0% of the time, Pallas kernels for 0%

commit v1 on v0

v1 whole, which is shorter than its diff:
```python
import functools
import math

import jax
import jax.numpy as jnp
from jax import lax
from jax.experimental import pallas as pl
from jax.experimental.pallas import tpu as pltpu
from jax.sharding import PartitionSpec as P

HD = 104
EPSILON = 1e-06
MESH = pl.DeviceIdType.MESH
RING = 8


def layer_norm(values, gains):
    average = jnp.mean(values, axis=-1, keepdims=True)
    centred = values - average
    variance = jnp.mean(centred * centred, axis=-1, keepdims=True)
    return centred * lax.rsqrt(variance + EPSILON) * gains


def rms_norm(values, gains):
    return values * lax.rsqrt(jnp.mean(values * values, axis=-1, keepdims=True) + EPSILON) * gains


def gelu(v):
    return 0.5 * v * (1.0 + lax.erf(v * math.sqrt(0.5)))


def slot_of(rel):
    if rel == 0:
        return 0
    if abs(rel) == 4:
        return 1
    return 2 * abs(rel) + (1 if rel > 0 else 0)


def vision_kernel(
    patch_ref, vg_ref, mg_ref, w1_hbm, w2_hbm, wm_hbm, out_ref,
    xg, acc, w1, w2, wm, rs_out, rs_in, fsend, frx, psend, prx, mg,
    local_sem, ws_sem, wr_sem, fs_sem, fr_sem, as_sem, ar_sem, rs_sem, rr_sem,
    ts_sem, tr_sem, ps_sem, pr_sem, gs_sem, gr_sem, xs_sem, xr_sem,
):
    r = lax.axis_index("req")
    t = lax.axis_index("tp")
    z = lax.rem(t, RING)
    xl = t // RING
    core = lax.rem(r, 2)
    xhi = lax.rem(r // 2, 2)
    inner = (r, (1 - xl) * RING + z)
    outer = (r + 2 - 4 * xhi, (1 - xl) * RING + z)
    sibling = (r + 1 - 2 * core, t)

    def column(k):
        return (r, xl * RING + lax.rem(z + k + RING, RING))

    rows = patch_ref.shape[0]
    half = rows // 2

    def remote(src, dst, ssem, rsem, dev):
        return pltpu.make_async_remote_copy(
            src_ref=src, dst_ref=dst, send_sem=ssem, recv_sem=rsem, device_id=dev, device_id_type=MESH
        )

    pending = []

    def send(src, dst, ssem, rsem, dev):
        c = remote(src, dst, ssem, rsem, dev)
        c.start()
        pending.append(c)
        return c

    barrier = pltpu.get_barrier_semaphore()
    peers = [column(k) for k in range(1, RING)] + [inner, outer, sibling]
    for dev in peers:
        pl.semaphore_signal(barrier, inc=1, device_id=dev, device_id_type=MESH)

    loads = [
        pltpu.make_async_copy(w1_hbm, w1.at[0], local_sem.at[0]),
        pltpu.make_async_copy(w2_hbm, w2.at[0], local_sem.at[1]),
        pltpu.make_async_copy(wm_hbm, wm.at[xl], local_sem.at[2]),
    ]
    for c in loads:
        c.start()

    wide = patch_ref[...].astype(jnp.float32)
    xg[0] = layer_norm(wide, vg_ref[...]).astype(jnp.bfloat16)
    pl.semaphore_wait(barrier, len(peers))

    ag = {}
    for d, s in ((0, 1), (1, -1)):
        ag[d, 0] = send(xg.at[0], xg.at[slot_of(-s)], as_sem.at[d, 0], ar_sem.at[d, 0], column(s))

    n1 = w1_hbm.shape[0] // 4
    n2 = w2_hbm.shape[0] // 4
    nm = wm_hbm.shape[0] // 2
    wx = []
    for i, dev in ((0, inner), (1, outer)):
        q = core * 2 + i
        a1 = pl.ds(pl.multiple_of(q * n1, 16), n1)
        a2 = pl.ds(pl.multiple_of(q * n2, 16), n2)
        wx.append((send(w1_hbm.at[a1], w1.at[1, a1], ws_sem.at[2 * i], wr_sem.at[2 * i], dev), w1.at[1, a1]))
        wx.append((send(w2_hbm.at[a2], w2.at[1, a2], ws_sem.at[2 * i + 1], wr_sem.at[2 * i + 1], dev), w2.at[1, a2]))
    am = pl.ds(pl.multiple_of(core * nm, 16), nm)
    wx.append((send(wm_hbm.at[am], wm.at[xl, am], ws_sem.at[4], wr_sem.at[4], inner), wm.at[1 - xl, am]))

    def mlp(pair, which):
        x = xg[2 * pair:2 * pair + 2].reshape(2 * rows, xg.shape[2])
        h = gelu(jnp.dot(x, w1[which], preferred_element_type=jnp.float32)).astype(jnp.bfloat16)
        return jnp.dot(h, w2[which], preferred_element_type=jnp.float32).reshape(2, rows, w2.shape[2])

    for step in range(4):
        for d, s in ((0, 1), (1, -1)):
            rel = -s * (step + 1)
            ag[d, step].wait_recv()
            if step < 3:
                src, dst = xg.at[slot_of(rel)], xg.at[slot_of(rel - s)]
                if step == 2:
                    part = pl.ds(d * half, half)
                    src, dst = src.at[part], dst.at[part]
                ag[d, step + 1] = send(src, dst, as_sem.at[d, step + 1], ar_sem.at[d, step + 1], column(s))
        if step == 0:
            loads[0].wait()
            loads[1].wait()
        pair = (step + 1) % 4
        acc[2 * pair:2 * pair + 2] = mlp(pair, 0)

    fwd = []
    for i, (c, ref) in enumerate(wx):
        c.wait_recv()
        fwd.append(send(ref, ref, fs_sem.at[i], fr_sem.at[i], sibling))
    for c in fwd[:4]:
        c.wait_recv()

    rs = {}
    for step in range(4):
        pair = (4 - step) % 4
        acc[2 * pair:2 * pair + 2] = acc[2 * pair:2 * pair + 2] + mlp(pair, 1)
        for d, s in ((0, 1), (1, -1)):
            block = acc.at[slot_of(s * (4 - step))]
            out = rs_out.at[d, step]
            if step == 0:
                part = pl.ds(d * half, half)
                out[part] = block[part].astype(jnp.bfloat16)
                rs[d, 0] = send(out.at[part], rs_in.at[d, 0, part], rs_sem.at[d, 0], rr_sem.at[d, 0], column(s))
                continue
            rs[d, step - 1].wait_recv()
            if step == 1:
                part = pl.ds(d * half, half)
                block[part] = block[part] + rs_in[d, 0, part].astype(jnp.float32)
                out[...] = block[...].astype(jnp.bfloat16)
            else:
                out[...] = (block[...] + rs_in[d, step - 1].astype(jnp.float32)).astype(jnp.bfloat16)
            rs[d, step] = send(out, rs_in.at[d, step], rs_sem.at[d, step], rr_sem.at[d, step], column(s))
    rs[0, 3].wait_recv()
    rs[1, 3].wait_recv()
    total = acc[0] + rs_in[0, 3].astype(jnp.float32) + rs_in[1, 3].astype(jnp.float32)
    nrm = layer_norm(patch_ref[...].astype(jnp.float32) + total, mg_ref[...]).astype(jnp.bfloat16)

    mrows = rows // 4
    width = wm_hbm.shape[0]
    to_row = lax.broadcasted_iota(jnp.int32, (rows, rows), 0)
    from_row = lax.broadcasted_iota(jnp.int32, (rows, rows), 1)
    order = (4 * (to_row % mrows) + to_row // mrows == from_row).astype(jnp.bfloat16)
    nrm = jnp.dot(order, nrm, preferred_element_type=jnp.float32).astype(jnp.bfloat16)
    for p in range(4):
        line = nrm[p * mrows:(p + 1) * mrows]
        for c in range(4):
            j = 4 * p + c
            fsend[j % RING, j // RING] = line[:, c * width:(c + 1) * width]
    a2a = []
    for k in range(1, RING):
        dest = lax.rem(z + k, RING)
        a2a.append(send(fsend.at[dest], frx.at[RING - k], ts_sem.at[k], tr_sem.at[k], column(k)))
    frx[0] = fsend[z]
    loads[2].wait()
    fwd[4].wait_recv()
    for c in a2a:
        c.wait_recv()

    part = jnp.dot(frx[:, 0].reshape(RING * mrows, width), wm[0], preferred_element_type=jnp.float32)
    part = part + jnp.dot(frx[:, 1].reshape(RING * mrows, width), wm[1], preferred_element_type=jnp.float32)
    psend[...] = part.reshape(psend.shape).astype(jnp.bfloat16)
    red = []
    for k in range(1, RING):
        red.append(send(psend.at[k], prx.at[RING - k], ps_sem.at[k], pr_sem.at[k], column(k)))
    total = part[:mrows]
    for c in red:
        c.wait_recv()
    for k in range(1, RING):
        total = total + prx[k].astype(jnp.float32)
    mg[t] = total.astype(jnp.bfloat16)

    gat, xfw = [], [send(mg.at[t], mg.at[t], xs_sem.at[0], xr_sem.at[0], inner)]
    for k in range(1, RING):
        gat.append(send(mg.at[t], mg.at[t], gs_sem.at[k], gr_sem.at[k], column(k)))
    for k in range(1, RING):
        src = xl * RING + lax.rem(z - k + RING, RING)
        gat[k - 1].wait_recv()
        xfw.append(send(mg.at[src], mg.at[src], xs_sem.at[k], xr_sem.at[k], inner))
    for c in xfw:
        c.wait_recv()
    out_ref[...] = mg[...].reshape(out_ref.shape)
    for c in pending:
        c.wait_send()


def vision(patches, vg, mgain, w1, w2, wm):
    rows, width = patches.shape
    hidden = w1.shape[1]
    mrows = rows // 4
    bf, f32 = jnp.bfloat16, jnp.float32
    dma = pltpu.SemaphoreType.DMA
    vmem = pl.BlockSpec(memory_space=pltpu.VMEM)
    hbm = pl.BlockSpec(memory_space=pl.ANY)
    return pl.pallas_call(
        vision_kernel,
        out_shape=jax.ShapeDtypeStruct((16 * mrows, width), bf),
        in_specs=[vmem] * 3 + [hbm] * 3,
        out_specs=vmem,
        scratch_shapes=[
            pltpu.VMEM((8, rows, width), bf),
            pltpu.VMEM((8, rows, width), f32),
            pltpu.VMEM((2, width, hidden), bf),
            pltpu.VMEM((2, hidden, width), bf),
            pltpu.VMEM((2, wm.shape[0], width), bf),
            pltpu.VMEM((2, 4, rows, width), bf),
            pltpu.VMEM((2, 4, rows, width), bf),
            pltpu.VMEM((8, 2, mrows, wm.shape[0]), bf),
            pltpu.VMEM((8, 2, mrows, wm.shape[0]), bf),
            pltpu.VMEM((8, mrows, width), bf),
            pltpu.VMEM((8, mrows, width), bf),
            pltpu.VMEM((16, mrows, width), bf),
            dma((3,)), dma((5,)), dma((5,)), dma((5,)), dma((5,)),
            dma((2, 4)), dma((2, 4)), dma((2, 4)), dma((2, 4)),
            dma((8,)), dma((8,)), dma((8,)), dma((8,)), dma((8,)), dma((8,)), dma((8,)), dma((8,)),
        ],
        compiler_params=pltpu.CompilerParams(
            collective_id=0, has_side_effects=True, vmem_limit_bytes=44 * 2**20
        ),
        cost_estimate=pl.CostEstimate(flops=200_000_000_000, bytes_accessed=50_000_000, transcendentals=0),
        name="vision",
    )(patches, vg, mgain, w1, w2, wm)


def attend(qkv_rows, doc_row):
    seq_len = qkv_rows.shape[0]
    block_rows = 256
    band = 1024
    queries = qkv_rows[:, :HD]
    pad = jnp.zeros((band - block_rows, HD), qkv_rows.dtype)
    key_rows = jnp.concatenate([pad, qkv_rows[:, HD:2 * HD]], axis=0)
    value_rows = jnp.concatenate([pad, qkv_rows[:, 2 * HD:]], axis=0)
    docs_pad = jnp.concatenate([jnp.full((band - block_rows,), -1, doc_row.dtype), doc_row])
    outs = []
    for start in range(0, seq_len, block_rows):
        q = queries[start:start + block_rows]
        k = key_rows[start:start + band]
        v = value_rows[start:start + band]
        qpos = start + jnp.arange(block_rows)
        kpos = start - (band - block_rows) + jnp.arange(band)
        allowed = (kpos[None, :] <= qpos[:, None]) & (
            docs_pad[None, start:start + band] == doc_row[start:start + block_rows, None]
        )
        scores = jnp.einsum("qe,ke->qk", q, k, preferred_element_type=jnp.float32) / math.sqrt(HD)
        scores = jnp.where(allowed, scores, -1e30)
        largest = jnp.max(scores, axis=-1, keepdims=True)
        raised = jnp.where(allowed, jnp.exp(scores - largest), 0.0)
        weights = (raised / jnp.sum(raised, axis=-1, keepdims=True)).astype(jnp.bfloat16)
        outs.append(jnp.dot(weights, v, preferred_element_type=jnp.float32).astype(jnp.bfloat16))
    return jnp.concatenate(outs, axis=0)


def shards(
    patches, vis_gain, w_fc1, w_fc2, merge_gain, w_merge, slots, text, docs, dec_gain, w_qkv, w_out
):
    slot_row = slots[0]
    text_rows = text[0]
    doc_row = docs[0]
    seq_here = text_rows.shape[0]
    text_in = rms_norm(text_rows.astype(jnp.float32), dec_gain).astype(jnp.bfloat16)
    text_all = lax.all_gather(text_in, "tp", axis=0, tiled=True)
    merged = vision(patches[0], vis_gain[None], merge_gain[None], w_fc1, w_fc2, w_merge)
    image_in = rms_norm(merged.astype(jnp.float32), dec_gain).astype(jnp.bfloat16)
    rows_in = text_all
    span = merged.shape[0] // 4
    for k in range(4):
        rows_in = lax.dynamic_update_slice_in_dim(
            rows_in, image_in[k * span:(k + 1) * span], slot_row[k * span], 0
        )
    qkv_rows = jnp.dot(rows_in, w_qkv, preferred_element_type=jnp.float32).astype(jnp.bfloat16)
    attended = attend(qkv_rows, doc_row)
    out_sum = lax.psum_scatter(
        jnp.dot(attended, w_out, preferred_element_type=jnp.float32).astype(jnp.bfloat16),
        "tp",
        scatter_dimension=0,
        tiled=True,
    ).astype(jnp.float32)
    positions = lax.axis_index("tp") * seq_here + jnp.arange(seq_here, dtype=jnp.int32)
    matches = slot_row[None, :] == positions[:, None]
    placed = jnp.dot(
        matches.astype(jnp.bfloat16), merged, preferred_element_type=jnp.float32
    ).astype(jnp.bfloat16)
    embedded = jnp.where(jnp.any(matches, axis=1)[:, None], placed, text_rows)
    decoded = (embedded.astype(jnp.float32) + out_sum).astype(jnp.bfloat16)
    return decoded[None]


def solution(mesh):
    placed = (
        P("req", "tp", None),
        P(),
        P(None, "tp"),
        P("tp", None),
        P(),
        P("tp", None),
        P("req", None),
        P("req", "tp", None),
        P("req", None),
        P(),
        P(None, "tp"),
        P("tp", None),
    )
    return jax.shard_map(
        shards, mesh=mesh, in_specs=placed, out_specs=P("req", "tp", None), check_vma=False
    )
```

time: 624 us -> 395 us (0.63)
  waiting for transfers between devices: 464 us -> 129 us
  Pallas kernels: 0 us -> 181 us
  matrix products: 68.8 us -> 27.7 us
  blocking collectives: 41 us -> 0 us
  between operations: 13.3 us -> 21.1 us
  local copies, waits for them, and re-layouts: 6.75 us -> 13.2 us
    all_gather x2 -> x1, waiting for transfers between devices: 203 us -> 0.02 us  [shards(): text_all = lax.all_gather(text_in, 'tp', axis=0, tiled=True)]
    pallas_call x0 -> x1, Pallas kernels: none -> 181 us  [vision(): pl.pallas_call(vision_kernel, out_shape=jax.ShapeDtypeStruct((16 * mrows,...]
    reduce_scatter x2 -> x0, waiting for transfers between devices: 144 us -> none  [the longest x1 75.1 us: shards(): lax.psum_scatter(jnp.dot(hidden, w_fc2, preferred_element_type=jnp.float3...]
    dot_general x15 -> x25, matrix products: 61.8 us -> 20 us  [the longest x1 7.57 us: shards(): jnp.dot(rows_in, w_qkv, preferred_element_type=jnp.float32)]
    all_gather x1 -> x0, blocking collectives: 30.6 us -> none  [shards(): merged = lax.all_gather(merged_share, 'tp', axis=0, tiled=True)]
    add x6 -> x22, other arithmetic: 0.02 us -> 12.6 us  [the longest x11 6.51 us: attend(): kpos = start - (band - block_rows) + jnp.arange(band)]
    reduce_sum x10 -> x13, other arithmetic: 19.7 us -> 7.14 us  [the longest x11 5.45 us: attend(): jnp.sum(raised, axis=-1, keepdims=True)]
    reduce_scatter x1, waiting for transfers between devices: 118 us -> 129 us  [shards(): lax.psum_scatter(jnp.dot(attended, w_out, preferred_element_type=jnp.floa...]
  transfers between devices with their start and end apart: 5 -> 2, of which waited for: 5 -> 1; matrix products, arithmetic and copies ran while one was open for 0% -> 4% of each run, Pallas kernels for 0% -> 46%
where the time goes in v1:
time: 395 us
  Pallas kernels  181 us (46%)
  waiting for transfers between devices  129 us (33%)
  matrix products  27.7 us (7%)
  other arithmetic  22.4 us (6%)
  between operations  21.1 us (5%)
  local copies, waits for them, and re-layouts  13.2 us (3%)
    pallas_call x1, Pallas kernels, vision(): pl.pallas_call(vision_kernel, out_shape=jax.ShapeDtypeStruct((16 * mrows,...  181 us
    reduce_scatter x1, waiting for transfers between devices, shards(): lax.psum_scatter(jnp.dot(attended, w_out, preferred_element_type=jnp.floa...  129 us
  transfers between devices with their start and end apart: 2, of which 1 were waited for; matrix products, arithmetic and copies ran while one was open for 4% of the time, Pallas kernels for 46%

profile of v1, /device:TPU:1, one launch (start us, length us, event | category | flops | bytes accessed | tf_op | source)
XLA Modules:
  0.0 394.7 jit_solution(15437090867670980638)
XLA Ops:
  6.6 1.4 fusion.20
  8.1 2.1 fusion.22
  10.3 0.6 fusion.126
  15.6 0.6 iota_add_fusion
  16.2 0.6 iota_add_fusion.11
  16.8 0.6 iota_add_fusion.1
  17.4 0.5 iota_add_fusion.12
  17.9 0.6 iota_add_fusion.2
  18.5 0.5 iota_add_fusion.13
  19.0 0.6 iota_add_fusion.3
  19.6 0.5 iota_add_fusion.14
  20.2 0.6 iota_add_fusion.4
  20.7 0.5 iota_add_fusion.15
  21.3 0.6 iota_add_fusion.5
  21.9 0.6 iota_add_fusion.16
  22.4 0.6 iota_add_fusion.6
  23.0 0.6 iota_add_fusion.17
  23.6 0.6 iota_add_fusion.7
  24.2 0.5 iota_add_fusion.18
  24.7 0.6 iota_add_fusion.19
  25.3 0.6 iota_add_fusion.8
  25.9 0.6 iota_add_fusion.20
  26.5 0.6 iota_add_fusion.9
  27.1 0.6 iota_add_fusion.21
  27.6 0.6 iota_add_fusion.10
  28.3 0.6 pad_slice_fusion.12
  31.3 1.4 copy-done.1
  32.7 1.5 copy-done.2
  34.2 181.5 %vision.1 = bf16[256,1664]{1,0:T(8,128)(2,1)S(1)} custom-call(bf16[64,1664]{1,0:T(8,128)(2,1)S(1)} %bitcast.39, f32[1,1664]{1,0:T(1,128)S(1)} %broadcast_in_dim.41.vg_ref, f32[1,1664]{1,0:T(1,128)S(1)} %broadcast_in_dim.42.mg_ref, bf16[1664,512]{1,0:T(8,128)(2,1)S(1)} %copy-done.1, bf16[512,1664]{1,0:T(8,128)(2,1)S(1)} %copy-done.2, ...), custom_call_target="tpu_custom_call" | custom-call | flops 199999995904 | bytes 50000000 | tf_op jit(solution)/shard_map/vision/pallas_call | solution.py:218
  216.4 1.8 dynamic_update_slice.12
  218.2 1.8 dynamic_update_slice.13
  220.0 1.8 dynamic_update_slice.14
  221.8 1.8 dynamic_update_slice.15
  223.5 7.6 %convolution_convert_fusion.1 = bf16[3072,312]{0,1:T(8,128)(2,1)S(1)} fusion(bf16[3072,1664]{1,0:T(8,128)(2,1)} %dynamic_update_slice.15, bf16[1664,312]{0,1:T(8,128)(2,1)S(1)} %copy-done), kind=kOutput, calls=%fused_computation.1 | convolution fusion | flops 3190726656 | bytes 13178880 | tf_op jit(solution)/shard_map/dot_general | solution.py:293
  231.3 0.6 copy-done.10
  231.8 0.5 fusion.138
  232.8 0.5 fusion.137
  233.8 0.5 fusion.136
  234.7 0.5 fusion.135
  235.7 0.5 fusion.134
  236.7 0.5 fusion.133
  237.6 0.5 fusion.132
  238.6 0.5 fusion.131
  239.6 0.5 fusion.130
  240.6 0.5 fusion.129
  241.6 0.5 fusion.127
  242.1 0.5 fusion.128
  242.6 1.0 fusion.37
  243.6 0.5 fusion.34
  244.1 0.6 fusion.33
  244.7 0.6 fusion.32
  245.2 0.6 fusion.31
  245.8 0.5 fusion.30
  246.3 0.5 fusion.29
  246.9 0.5 fusion.28
  247.4 0.5 fusion.27
  248.0 0.5 fusion.26
  248.5 0.5 fusion.25
  249.1 0.5 fusion.24
  249.6 0.5 fusion.23
  250.6 5.4 %convolution_convert_fusion = bf16[3072,1664]{1,0:T(8,128)(2,1)} fusion(bf16[3072,104]{1,0:T(8,128)(2,1)S(1)} %fusion.23, bf16[104,1664]{1,0:T(8,128)(2,1)S(1)} %copy-done.6), kind=kOutput, calls=%fused_computation | convolution fusion | flops 1068367872 | bytes 11208704 | tf_op jit(solution)/shard_map/dot_general | solution.py:296
  256.0 0.6 copy-done.25
  256.8 128.6 %reduce-scatter.2.cloned.1.call-done = bf16[192,1664]{1,0:T(8,128)(2,1)} async-done(((bf16[3072,1664]{1,0:T(8,128)(2,1)}), bf16[192,1664]{1,0:T(8,128)(2,1)}) %reduce-scatter.2.cloned.1.call-update) | async-done | bytes 638992 | tf_op jit(solution)/shard_map/reduce_scatter | solution.py:295
  385.5 2.4 fusion.4
  (101 shorter events, 6.1 us)
Async XLA Ops:
  6.5 217.0 %copy-start = (bf16[1664,312]{0,1:T(8,128)(2,1)S(1)}, bf16[1664,312]{0,1:T(8,128)(2,1)}, u32[]{:S(2)}) copy-start(bf16[1664,312]{0,1:T(8,128)(2,1)} %param.22) | copy-start | bytes 3115012
  6.5 3.7 copy-start.24
  6.5 21.7 %copy-start.26 = (f32[1664]{0:T(1024)S(1)}, f32[1664]{0:T(1024)}, u32[]{:S(2)}) copy-start(f32[1664]{0:T(1024)} %param.13) | copy-start | bytes 19972
  6.5 21.7 %copy-start.27 = (f32[1664]{0:T(1024)S(1)}, f32[1664]{0:T(1024)}, u32[]{:S(2)}) copy-start(f32[1664]{0:T(1024)} %param.16) | copy-start | bytes 19972
  6.5 21.7 %copy-start.7 = (s32[1,3072]{1,0:T(1,128)S(1)}, s32[1,3072]{1,0:T(1,128)}, u32[]{:S(2)}) copy-start(s32[1,3072]{1,0:T(1,128)} %param.20) | copy-start | bytes 36868
  6.6 24.7 %copy-start.4 = (bf16[1,64,1664]{2,1,0:T(8,128)(2,1)S(1)}, bf16[1,64,1664]{2,1,0:T(8,128)(2,1)}, u32[]{:S(2)}) copy-start(bf16[1,64,1664]{2,1,0:T(8,128)(2,1)} %param.12) | copy-start | bytes 638980
  6.6 24.7 %copy-start.3 = (bf16[416,1664]{1,0:T(8,128)(2,1)S(1)}, bf16[416,1664]{1,0:T(8,128)(2,1)}, u32[]{:S(2)}) copy-start(bf16[416,1664]{1,0:T(8,128)(2,1)} %wm_hbm.1) | copy-start | bytes 4153348
  6.6 209.8 %all-gather.2.cloned.1.call-start = ((), (), s32[]{:S(2)}) async-start(), calls=%async_computation.1 | async-start | bytes 10862592 | tf_op jit(solution)/shard_map/all_gather | solution.py:284
  10.2 375.2 %reduce-scatter.2.cloned.1.call-start = ((), (), s32[]{:S(2)}) async-start(), calls=%async_computation.2 | async-start | bytes 10862592 | tf_op jit(solution)/shard_map/reduce_scatter | solution.py:295
  31.3 1.5 copy-start.1
  32.7 1.5 copy-start.2
  34.2 181.8 %copy-start.8 = (s32[1,3072]{1,0:T(1,128)S(1)}, s32[1,3072]{1,0:T(1,128)}, u32[]{:S(2)}) copy-start(s32[1,3072]{1,0:T(1,128)} %param.20) | copy-start | bytes 36868
  34.2 181.8 %copy-start.9 = (f32[1664]{0:T(1024)S(1)}, f32[1664]{0:T(1024)}, u32[]{:S(2)}) copy-start(f32[1664]{0:T(1024)} %param.21) | copy-start | bytes 19972
  231.1 0.7 copy-start.10
  231.1 0.7 copy-start.29
  231.2 1.5 copy-start.11
  231.2 1.5 copy-start.30
  232.3 1.4 copy-start.12
  232.3 1.4 copy-start.31
  233.3 1.4 copy-start.13
  233.3 1.4 copy-start.32
  234.2 1.4 copy-start.14
  234.3 1.4 copy-start.33
  235.2 1.4 copy-start.15
  235.2 1.4 copy-start.34
  236.2 1.4 copy-start.16
  236.2 1.4 copy-start.35
  237.2 1.4 copy-start.17
  237.2 1.4 copy-start.36
  238.1 1.4 copy-start.37
  239.1 1.5 copy-start.18
  239.1 1.5 copy-start.21
  239.1 1.5 copy-start.38
  240.1 1.5 copy-start.20
  240.1 1.5 copy-start.23
  241.1 1.0 copy-start.19
  241.1 1.0 copy-start.22
  241.1 1.0 copy-start.28
  249.6 1.0 copy-start.6
  255.9 0.7 copy-start.25
  256.0 129.5 %copy-start.5 = (bf16[1,192,1664]{2,1,0:T(8,128)(2,1)S(1)}, bf16[1,192,1664]{2,1,0:T(8,128)(2,1)}, u32[]{:S(2)}) copy-start(bf16[1,192,1664]{2,1,0:T(8,128)(2,1)} %param.19) | copy-start | bytes 1916932
Sparse Core Ops, SparseCore 0:
  10.3 146.7 all-gather.1
  256.1 129.3 reduce-scatter.1

commit v2 on v1

--- a/solution.py
+++ b/solution.py
@@ -38,10 +38,12 @@
 
 
 def vision_kernel(
-    patch_ref, vg_ref, mg_ref, w1_hbm, w2_hbm, wm_hbm, out_ref,
-    xg, acc, w1, w2, wm, rs_out, rs_in, fsend, frx, psend, prx, mg,
+    patch_ref, vg_ref, mg_ref, text_ref, dg_ref, w1_hbm, w2_hbm, wm_hbm, wc_hbm,
+    out_ref, win, wg,
+    ti, xg, acc, w1, w2, wm, rs_out, rs_in, fsend, frx, psend, prx, mg,
     local_sem, ws_sem, wr_sem, fs_sem, fr_sem, as_sem, ar_sem, rs_sem, rr_sem,
     ts_sem, tr_sem, ps_sem, pr_sem, gs_sem, gr_sem, xs_sem, xr_sem,
+    zs_sem, zr_sem, ys_sem, yr_sem, y2s_sem, y2r_sem, os_sem, or_sem, ss_sem, sr_sem, hs_sem, hr_sem,
 ):
     r = lax.axis_index("req")
     t = lax.axis_index("tp")
@@ -53,6 +55,10 @@
     outer = (r + 2 - 4 * xhi, (1 - xl) * RING + z)
     sibling = (r + 1 - 2 * core, t)
 
+    tp_size = 2 * RING
+    after, before = (r, lax.rem(t + 1, tp_size)), (r, lax.rem(t + tp_size - 1, tp_size))
+    y_next, y_prev = (lax.rem(r + 4, 16), t), (lax.rem(r + 12, 16), t)
+
     def column(k):
         return (r, xl * RING + lax.rem(z + k + RING, RING))
 
@@ -73,11 +79,12 @@
         return c
 
     barrier = pltpu.get_barrier_semaphore()
-    peers = [column(k) for k in range(1, RING)] + [inner, outer, sibling]
+    peers = [column(k) for k in range(1, RING)] + [inner, outer, sibling, after, before, y_next, y_prev]
     for dev in peers:
         pl.semaphore_signal(barrier, inc=1, device_id=dev, device_id_type=MESH)
 
     loads = [
+        pltpu.make_async_copy(wc_hbm, wg.at[t], local_sem.at[3]),
         pltpu.make_async_copy(w1_hbm, w1.at[0], local_sem.at[0]),
         pltpu.make_async_copy(w2_hbm, w2.at[0], local_sem.at[1]),
         pltpu.make_async_copy(wm_hbm, wm.at[xl], local_sem.at[2]),
@@ -106,6 +113,72 @@
     am = pl.ds(pl.multiple_of(core * nm, 16), nm)
     wx.append((send(wm_hbm.at[am], wm.at[xl, am], ws_sem.at[4], wr_sem.at[4], inner), wm.at[1 - xl, am]))
 
+    quarter = wc_hbm.shape[0] // 4
+    y = r // 4
+    s_w = 1 - 2 * core
+    ahead = column(s_w)
+
+    def quarter_at(k):
+        return pl.ds(pl.multiple_of(lax.rem(y + k, 4) * quarter, 8), quarter)
+
+    def shard_at(k):
+        return xl * RING + lax.rem(z - s_w * (k + 1) + RING, RING)
+
+    zc = [send(wc_hbm.at[quarter_at(0)], wg.at[t, quarter_at(0)], zs_sem.at[0], zr_sem.at[0], ahead)]
+    yc, y2c, xc, sc, hc = {}, {}, {}, [], []
+
+    def from_column(k):
+        piece = wg.at[shard_at(k), quarter_at(0)]
+        zc[k].wait_recv()
+        if k < 3:
+            zc.append(send(piece, piece, zs_sem.at[k + 1], zr_sem.at[k + 1], ahead))
+        yc[k] = (
+            send(piece, piece, ys_sem.at[k, 0], yr_sem.at[k, 0], y_next),
+            send(piece, piece, ys_sem.at[k, 1], yr_sem.at[k, 1], y_prev),
+        )
+
+    def from_y(k):
+        for c in yc[k]:
+            c.wait_recv()
+        piece = wg.at[shard_at(k), quarter_at(3 if k % 2 == 0 else 1)]
+        y2c[k] = send(piece, piece, y2s_sem.at[k], y2r_sem.at[k], y_next if k % 2 == 0 else y_prev)
+
+    def both_halves(ref, i):
+        n = wc_hbm.shape[0] // 2
+        return ref.at[pl.ds(i * n, n)]
+
+    def to_x(k):
+        y2c[k].wait_recv()
+        if k == 3:
+            loads[0].wait()
+            idx = xl * RING + lax.rem(z + 4 - 4 * core, RING)
+        else:
+            idx = shard_at(k)
+        xc[k] = [
+            send(both_halves(wg.at[idx], i), both_halves(wg.at[idx], i), os_sem.at[k, i], or_sem.at[k, i], dev)
+            for i, dev in ((0, inner), (1, outer))
+        ]
+        if k < 3:
+            sc.append(send(wg.at[idx], wg.at[idx], ss_sem.at[k], sr_sem.at[k], sibling))
+
+    def from_x(k):
+        if k == 3:
+            idx = lax.rem(z + 4 - 4 * core, RING)
+        else:
+            idx = lax.rem(z - s_w * (k + 1) + RING, RING)
+        idx = (1 - xl) * RING + idx
+        for c in xc[k]:
+            c.wait_recv()
+        sc.append(send(wg.at[idx], wg.at[idx], ss_sem.at[3 + k], sr_sem.at[3 + k], sibling))
+
+    def window(k):
+        if k == 0:
+            hc.append(send(ti, win.at[1], hs_sem.at[0], hr_sem.at[0], after))
+            return
+        hc[k - 1].wait_recv()
+        if k < 4:
+            hc.append(send(win.at[k], win.at[k + 1], hs_sem.at[k], hr_sem.at[k], after))
+
     def mlp(pair, which):
         x = xg[2 * pair:2 * pair + 2].reshape(2 * rows, xg.shape[2])
         h = gelu(jnp.dot(x, w1[which], preferred_element_type=jnp.float32)).astype(jnp.bfloat16)
@@ -122,10 +195,19 @@
                     src, dst = src.at[part], dst.at[part]
                 ag[d, step + 1] = send(src, dst, as_sem.at[d, step + 1], ar_sem.at[d, step + 1], column(s))
         if step == 0:
-            loads[0].wait()
             loads[1].wait()
+            loads[2].wait()
         pair = (step + 1) % 4
         acc[2 * pair:2 * pair + 2] = mlp(pair, 0)
+        from_column(step)
+        if step >= 1:
+            from_y(step - 1)
+        if step >= 2:
+            to_x(step - 2)
+    ti[...] = rms_norm(text_ref[...].astype(jnp.float32), dg_ref[...]).astype(jnp.bfloat16)
+    own_window = pltpu.make_async_copy(ti, win.at[0], local_sem.at[4])
+    own_window.start()
+    window(0)
 
     fwd = []
     for i, (c, ref) in enumerate(wx):
@@ -154,6 +236,16 @@
             else:
                 out[...] = (block[...] + rs_in[d, step - 1].astype(jnp.float32)).astype(jnp.bfloat16)
             rs[d, step] = send(out, rs_in.at[d, step], rs_sem.at[d, step], rr_sem.at[d, step], column(s))
+        if step == 0:
+            from_y(3)
+            to_x(2)
+        if step == 1:
+            to_x(3)
+            from_x(0)
+        if step == 2:
+            window(1)
+        if step == 3:
+            from_x(1)
     rs[0, 3].wait_recv()
     rs[1, 3].wait_recv()
     total = acc[0] + rs_in[0, 3].astype(jnp.float32) + rs_in[1, 3].astype(jnp.float32)
@@ -175,7 +267,8 @@
         dest = lax.rem(z + k, RING)
         a2a.append(send(fsend.at[dest], frx.at[RING - k], ts_sem.at[k], tr_sem.at[k], column(k)))
     frx[0] = fsend[z]
-    loads[2].wait()
+    window(2)
+    loads[3].wait()
     fwd[4].wait_recv()
     for c in a2a:
         c.wait_recv()
@@ -186,6 +279,7 @@
     red = []
     for k in range(1, RING):
         red.append(send(psend.at[k], prx.at[RING - k], ps_sem.at[k], pr_sem.at[k], column(k)))
+    from_x(2)
     total = part[:mrows]
     for c in red:
         c.wait_recv()
@@ -196,6 +290,8 @@
     gat, xfw = [], [send(mg.at[t], mg.at[t], xs_sem.at[0], xr_sem.at[0], inner)]
     for k in range(1, RING):
         gat.append(send(mg.at[t], mg.at[t], gs_sem.at[k], gr_sem.at[k], column(k)))
+    window(3)
+    from_x(3)
     for k in range(1, RING):
         src = xl * RING + lax.rem(z - k + RING, RING)
         gat[k - 1].wait_recv()
@@ -203,11 +299,15 @@
     for c in xfw:
         c.wait_recv()
     out_ref[...] = mg[...].reshape(out_ref.shape)
+    window(4)
+    own_window.wait()
+    for c in sc:
+        c.wait_recv()
     for c in pending:
         c.wait_send()
 
 
-def vision(patches, vg, mgain, w1, w2, wm):
+def vision(patches, vg, mgain, text, dgain, w1, w2, wm, wc):
     rows, width = patches.shape
     hidden = w1.shape[1]
     mrows = rows // 4
@@ -217,10 +317,15 @@
     hbm = pl.BlockSpec(memory_space=pl.ANY)
     return pl.pallas_call(
         vision_kernel,
-        out_shape=jax.ShapeDtypeStruct((16 * mrows, width), bf),
-        in_specs=[vmem] * 3 + [hbm] * 3,
-        out_specs=vmem,
+        out_shape=(
+            jax.ShapeDtypeStruct((16 * mrows, width), bf),
+            jax.ShapeDtypeStruct((5, text.shape[0], width), bf),
+            jax.ShapeDtypeStruct((16, wc.shape[0], width), bf),
+        ),
+        in_specs=[vmem] * 5 + [hbm] * 4,
+        out_specs=(vmem, hbm, hbm),
         scratch_shapes=[
+            pltpu.VMEM(text.shape, bf),
             pltpu.VMEM((8, rows, width), bf),
             pltpu.VMEM((8, rows, width), f32),
             pltpu.VMEM((2, width, hidden), bf),
@@ -233,79 +338,105 @@
             pltpu.VMEM((8, mrows, width), bf),
             pltpu.VMEM((8, mrows, width), bf),
             pltpu.VMEM((16, mrows, width), bf),
-            dma((3,)), dma((5,)), dma((5,)), dma((5,)), dma((5,)),
+            dma((5,)), dma((5,)), dma((5,)), dma((5,)), dma((5,)),
             dma((2, 4)), dma((2, 4)), dma((2, 4)), dma((2, 4)),
             dma((8,)), dma((8,)), dma((8,)), dma((8,)), dma((8,)), dma((8,)), dma((8,)), dma((8,)),
+            dma((4,)), dma((4,)), dma((4, 2)), dma((4, 2)), dma((4,)), dma((4,)),
+            dma((4, 2)), dma((4, 2)), dma((7,)), dma((7,)), dma((4,)), dma((4,)),
         ],
         compiler_params=pltpu.CompilerParams(
-            collective_id=0, has_side_effects=True, vmem_limit_bytes=44 * 2**20
+            collective_id=0, has_side_effects=True, vmem_limit_bytes=56 * 2**20
         ),
-        cost_estimate=pl.CostEstimate(flops=200_000_000_000, bytes_accessed=50_000_000, transcendentals=0),
+        cost_estimate=pl.CostEstimate(flops=100_000_000_000, bytes_accessed=50_000_000, transcendentals=0),
         name="vision",
-    )(patches, vg, mgain, w1, w2, wm)
-
-
-def attend(qkv_rows, doc_row):
-    seq_len = qkv_rows.shape[0]
-    block_rows = 256
-    band = 1024
-    queries = qkv_rows[:, :HD]
-    pad = jnp.zeros((band - block_rows, HD), qkv_rows.dtype)
-    key_rows = jnp.concatenate([pad, qkv_rows[:, HD:2 * HD]], axis=0)
-    value_rows = jnp.concatenate([pad, qkv_rows[:, 2 * HD:]], axis=0)
-    docs_pad = jnp.concatenate([jnp.full((band - block_rows,), -1, doc_row.dtype), doc_row])
-    outs = []
-    for start in range(0, seq_len, block_rows):
-        q = queries[start:start + block_rows]
-        k = key_rows[start:start + band]
-        v = value_rows[start:start + band]
-        qpos = start + jnp.arange(block_rows)
-        kpos = start - (band - block_rows) + jnp.arange(band)
-        allowed = (kpos[None, :] <= qpos[:, None]) & (
-            docs_pad[None, start:start + band] == doc_row[start:start + block_rows, None]
-        )
-        scores = jnp.einsum("qe,ke->qk", q, k, preferred_element_type=jnp.float32) / math.sqrt(HD)
-        scores = jnp.where(allowed, scores, -1e30)
-        largest = jnp.max(scores, axis=-1, keepdims=True)
-        raised = jnp.where(allowed, jnp.exp(scores - largest), 0.0)
-        weights = (raised / jnp.sum(raised, axis=-1, keepdims=True)).astype(jnp.bfloat16)
-        outs.append(jnp.dot(weights, v, preferred_element_type=jnp.float32).astype(jnp.bfloat16))
-    return jnp.concatenate(outs, axis=0)
+    )(patches, vg, mgain, text, dgain, w1, w2, wm, wc)
+
+
+NT = (((1,), (1,)), ((), ()))
+
+
+def decode_kernel(
+    win_ref, merged_ref, text_ref, gain_ref, slot_ref, kcol_ref, krow_ref, dcol_ref, drow_ref, w_ref, out_ref,
+    x, acc, bias,
+):
+    bf, f32 = jnp.bfloat16, jnp.float32
+    rows = text_ref.shape[0]
+    block = w_ref.shape[0] // 2
+
+    @pl.when(pl.program_id(0) == 0)
+    def _():
+        match = kcol_ref[...] == slot_ref[...]
+        onehot = match.astype(f32)
+        hit = jnp.max(onehot, axis=1, keepdims=True) > 0.0
+        onehot = onehot.astype(bf)
+        image = rms_norm(merged_ref[...].astype(f32), gain_ref[...]).astype(bf)
+        placed = jnp.dot(onehot, image, preferred_element_type=f32)
+        x[...] = jnp.where(hit, placed, win_ref[...].astype(f32)).astype(bf)
+        placed = jnp.dot(onehot[:rows], merged_ref[...], preferred_element_type=f32)
+        acc[...] = jnp.where(hit[:rows], placed, text_ref[...].astype(f32))
+        allowed = (krow_ref[...] <= kcol_ref[:rows, :]) & (drow_ref[...] == dcol_ref[...])
+        bias[...] = jnp.where(allowed, 0.0, -1e30)
+
+    lane = lax.broadcasted_iota(jnp.int32, (rows, block), 1)
+    kv = lax.dot_general(x[...], w_ref[:block], NT, preferred_element_type=f32).astype(bf)
+    q = lax.dot_general(x[:rows], w_ref[block:], NT, preferred_element_type=f32)
+    q = jnp.where(lane < HD, q, 0.0).astype(bf)
+    scores = lax.dot_general(q, kv, NT, preferred_element_type=f32) * (1.0 / math.sqrt(HD)) + bias[...]
+    raised = jnp.exp(scores - jnp.max(scores, axis=1, keepdims=True))
+    total = jnp.sum(raised, axis=1, keepdims=True)
+    mixed = jnp.dot(raised.astype(bf), kv, preferred_element_type=f32) / total
+    mixed = jnp.where(lane < HD, 0.0, mixed).astype(bf)
+    acc[...] += jnp.dot(mixed, w_ref[block:], preferred_element_type=f32)
+
+    @pl.when(pl.program_id(0) == pl.num_programs(0) - 1)
+    def _():
+        out_ref[...] = acc[...].astype(bf)
+
+
+def decode(win, merged, text, gain, slots, kcol, krow, dcol, drow, wg):
+    heads, depth, width = wg.shape
+    rows = text.shape[0]
+    span = win.shape[0]
+
+    def whole(a):
+        return pl.BlockSpec(a.shape, lambda h: (0,) * a.ndim)
+
+    args = (win, merged, text, gain, slots, kcol, krow, dcol, drow)
+    return pl.pallas_call(
+        decode_kernel,
+        grid=(heads,),
+        out_shape=jax.ShapeDtypeStruct((rows, width), jnp.bfloat16),
+        in_specs=[whole(a) for a in args] + [pl.BlockSpec((None, depth, width), lambda h: (h, 0, 0))],
+        out_specs=pl.BlockSpec((rows, width), lambda h: (0, 0)),
+        scratch_shapes=[
+            pltpu.VMEM((span, width), jnp.bfloat16),
+            pltpu.VMEM((rows, width), jnp.float32),
+            pltpu.VMEM((rows, span), jnp.float32),
+        ],
+        compiler_params=pltpu.CompilerParams(vmem_limit_bytes=50 * 2**20),
+        name="decode",
+    )(*args, wg)
 
 
 def shards(
     patches, vis_gain, w_fc1, w_fc2, merge_gain, w_merge, slots, text, docs, dec_gain, w_qkv, w_out
 ):
-    slot_row = slots[0]
     text_rows = text[0]
-    doc_row = docs[0]
-    seq_here = text_rows.shape[0]
-    text_in = rms_norm(text_rows.astype(jnp.float32), dec_gain).astype(jnp.bfloat16)
-    text_all = lax.all_gather(text_in, "tp", axis=0, tiled=True)
-    merged = vision(patches[0], vis_gain[None], merge_gain[None], w_fc1, w_fc2, w_merge)
-    image_in = rms_norm(merged.astype(jnp.float32), dec_gain).astype(jnp.bfloat16)
-    rows_in = text_all
-    span = merged.shape[0] // 4
-    for k in range(4):
-        rows_in = lax.dynamic_update_slice_in_dim(
-            rows_in, image_in[k * span:(k + 1) * span], slot_row[k * span], 0
-        )
-    qkv_rows = jnp.dot(rows_in, w_qkv, preferred_element_type=jnp.float32).astype(jnp.bfloat16)
-    attended = attend(qkv_rows, doc_row)
-    out_sum = lax.psum_scatter(
-        jnp.dot(attended, w_out, preferred_element_type=jnp.float32).astype(jnp.bfloat16),
-        "tp",
-        scatter_dimension=0,
-        tiled=True,
-    ).astype(jnp.float32)
-    positions = lax.axis_index("tp") * seq_here + jnp.arange(seq_here, dtype=jnp.int32)
-    matches = slot_row[None, :] == positions[:, None]
-    placed = jnp.dot(
-        matches.astype(jnp.bfloat16), merged, preferred_element_type=jnp.float32
-    ).astype(jnp.bfloat16)
-    embedded = jnp.where(jnp.any(matches, axis=1)[:, None], placed, text_rows)
-    decoded = (embedded.astype(jnp.float32) + out_sum).astype(jnp.bfloat16)
-    return decoded[None]
+    rows = text_rows.shape[0]
+    across = w_qkv.T
+    wc = jnp.concatenate([across[HD:], across[:HD], w_out], axis=0)
+    merged, win, wg = vision(
+        patches[0], vis_gain[None], merge_gain[None], text_rows, dec_gain[None], w_fc1, w_fc2, w_merge, wc
+    )
+    t = lax.axis_index("tp")
+    doc_pad = jnp.concatenate([jnp.full((4 * rows,), -1, jnp.int32), docs[0]])
+    doc_win = lax.dynamic_slice_in_dim(doc_pad, t * rows, 5 * rows, 0).reshape(5, rows)[::-1].reshape(-1)
+    pos = ((t - jnp.arange(5, dtype=jnp.int32))[:, None] * rows + jnp.arange(rows, dtype=jnp.int32)).reshape(-1)
+    out = decode(
+        win.reshape(5 * rows, -1), merged, text_rows, dec_gain[None], slots,
+        pos[:, None], pos[None], doc_win[:rows, None], doc_win[None], wg,
+    )
+    return out[None]
 
 
 def solution(mesh):

time: 395 us -> 232 us (0.59)
  waiting for transfers between devices: 129 us -> 0 us
  Pallas kernels: 181 us -> 220 us
  matrix products: 27.7 us -> 0 us
  other arithmetic: 22.4 us -> 1.34 us
  between operations: 21.1 us -> 0.08 us
  local copies, waits for them, and re-layouts: 13.2 us -> 8.09 us
    reduce_scatter x1 -> x0, waiting for transfers between devices: 129 us -> none  [shards(): lax.psum_scatter(jnp.dot(attended, w_out, preferred_element_type=jnp.floa...]
    pallas_call x1 -> x2, Pallas kernels: 181 us -> 220 us  [the longest x1 172 us: vision(): pl.pallas_call(vision_kernel, out_shape=(jax.ShapeDtypeStruct((16 * mrows...]
    dot_general x27 -> x0, matrix products: 27.7 us -> none  [the longest x1 7.57 us: shards(): jnp.dot(rows_in, w_qkv, preferred_element_type=jnp.float32)]
    add x23 -> x1, other arithmetic: 12.6 us -> 0.07 us  [shards(): (t - jnp.arange(5, dtype=jnp.int32))[:, None] * rows]
    dynamic_update_slice x4 -> x0, local copies, waits for them, and re-layouts: 7.14 us -> none  [shards(): lax.dynamic_update_slice_in_dim(rows_in, image_in[k * span:(k + 1) * span...]
    reduce_sum x13 -> x0, other arithmetic: 7.14 us -> none  [the longest x11 5.45 us: attend(): jnp.sum(raised, axis=-1, keepdims=True)]
  transfers between devices with their start and end apart: 2 -> 0, of which waited for: 1 -> 0; matrix products, arithmetic and copies ran while one was open for 4% -> 0% of each run, Pallas kernels for 46% -> 0%
where the time goes in v2:
time: 232 us; the launch traced here: 230 us
  Pallas kernels  220 us (95%)
  local copies, waits for them, and re-layouts  8.09 us (3%)
    pallas_call x1, Pallas kernels, vision(): pl.pallas_call(vision_kernel, out_shape=(jax.ShapeDtypeStruct((16 * mrows...  172 us
    pallas_call x1, Pallas kernels, decode(): pl.pallas_call(decode_kernel, grid=(heads,), out_shape=jax.ShapeDtypeStru...  48.4 us

profile of v2, /device:TPU:1, one launch (start us, length us, event | category | flops | bytes accessed | tf_op | source)
XLA Modules:
  0.0 229.7 jit_solution(8991769236502096278)
XLA Ops:
  0.0 0.0 copy-start.4
  0.0 1.3 broadcast_in_dim.19.vg_ref
  1.3 1.3 broadcast_in_dim.20.mg_ref
  2.6 1.3 broadcast_in_dim.21.dg_ref.gain_ref
  3.9 1.0 slice.16
  5.0 1.2 slice.15
  6.1 0.0 copy-done.4
  6.1 1.3 pad_maximum_fusion.wc_hbm
  7.4 0.0 copy-start.5
  7.4 0.0 copy-start.1
  7.4 0.0 copy-start.2
  7.4 0.0 copy-start.3
  7.4 171.8 %vision.1 = (bf16[256,1664]{1,0:T(8,128)(2,1)}, bf16[5,192,1664]{2,1,0:T(8,128)(2,1)}, bf16[16,416,1664]{2,1,0:T(8,128)(2,1)}) custom-call(bf16[64,1664]{1,0:T(8,128)(2,1)} %bitcast.14, f32[1,1664]{1,0:T(1,128)} %broadcast_in_dim.19.vg_ref, f32[1,1664]{1,0:T(1,128)} %broadcast_in_dim.20.mg_ref, bf16[192,1664]{1,0:T(8,128)(2,1)} %bitcast.7, ...), custom_call_target="tpu_custom_call" | custom-call | flops 99999997952 | bytes 50000000 | tf_op jit(solution)/shard_map/vision/pallas_call | solution.py:318
  179.2 0.1 iota_add_fusion
  179.3 0.4 add.44.kcol_ref
  179.6 0.1 add.42.krow_ref
  179.7 0.0 copy-done.5
  179.7 0.1 pad_dynamic-slice_fusion
  179.8 0.1 copy.14.dcol_ref
  179.9 0.1 reshape.62
  180.0 0.1 broadcast_in_dim_reshape.2.drow_ref
  180.1 0.0 copy-done.1
  180.1 0.0 copy-done.2
  180.1 0.0 copy-done.3
  180.1 0.0 copy-start
  180.1 1.1 copy-done
  181.3 48.4 %decode.1 = bf16[192,1664]{1,0:T(8,128)(2,1)} custom-call(bf16[960,1664]{1,0:T(8,128)(2,1)} %bitcast.9, bf16[256,1664]{1,0:T(8,128)(2,1)S(1)} %copy-done, bf16[192,1664]{1,0:T(8,128)(2,1)S(1)} %bitcast.8, f32[1,1664]{1,0:T(1,128)S(1)} %copy-done.2, s32[1,256]{1,0:T(1,128)S(1)} %copy-done.3, s32[960,1]{1,0:T(8,128)S(1)} %add.44.kcol_ref, ...), custom_call_target="tpu_custom_call" | custom-call | tf_op jit(solution)/shard_map/decode/pallas_call | solution.py:405
  (3 shorter events, 0.1 us)
Async XLA Ops:
  0.0 6.1 %copy-start.4 = (bf16[104,1664]{1,0:T(8,128)(2,1)S(1)}, bf16[104,1664]{1,0:T(8,128)(2,1)}, u32[]{:S(2)}) copy-start(bf16[104,1664]{1,0:T(8,128)(2,1)} %param.23) | copy-start | bytes 1038340
  7.4 172.3 %copy-start.5 = (s32[1,3072]{1,0:T(1,128)S(1)}, s32[1,3072]{1,0:T(1,128)}, u32[]{:S(2)}) copy-start(s32[1,3072]{1,0:T(1,128)} %param.20) | copy-start | bytes 36868
  7.4 172.7 %copy-start.1 = (bf16[1,192,1664]{2,1,0:T(8,128)(2,1)S(1)}, bf16[1,192,1664]{2,1,0:T(8,128)(2,1)}, u32[]{:S(2)}) copy-start(bf16[1,192,1664]{2,1,0:T(8,128)(2,1)} %param.19) | copy-start | bytes 1916932
  7.4 172.7 %copy-start.2 = (f32[1,1664]{1,0:T(1,128)S(1)}, f32[1,1664]{1,0:T(1,128)}, u32[]{:S(2)}) copy-start(f32[1,1664]{1,0:T(1,128)} %broadcast_in_dim.21.dg_ref.gain_ref) | copy-start | bytes 19972
  7.4 172.7 %copy-start.3 = (s32[1,256]{1,0:T(1,128)S(1)}, s32[1,256]{1,0:T(1,128)}, u32[]{:S(2)}) copy-start(s32[1,256]{1,0:T(1,128)} %slot_ref.1) | copy-start | bytes 3076
  180.1 1.2 copy-start

commit v3 on v2

--- a/solution.py
+++ b/solution.py
@@ -38,12 +38,12 @@
 
 
 def vision_kernel(
-    patch_ref, vg_ref, mg_ref, text_ref, dg_ref, w1_hbm, w2_hbm, wm_hbm, wc_hbm,
-    out_ref, win, wg,
-    ti, xg, acc, w1, w2, wm, rs_out, rs_in, fsend, frx, psend, prx, mg,
+    patch_ref, text_ref, gain_ref, slot_ref, dcol_ref, drow_ref, w1_hbm, w2_hbm, wm_hbm, wc_hbm,
+    out_ref,
+    win, wg, bias, total, xg, acc, w1, w2, wm, rs_out, rs_in, fsend, frx, psend, prx, mg, mine,
     local_sem, ws_sem, wr_sem, fs_sem, fr_sem, as_sem, ar_sem, rs_sem, rr_sem,
-    ts_sem, tr_sem, ps_sem, pr_sem, gs_sem, gr_sem, xs_sem, xr_sem,
-    zs_sem, zr_sem, ys_sem, yr_sem, y2s_sem, y2r_sem, os_sem, or_sem, ss_sem, sr_sem, hs_sem, hr_sem,
+    ts_sem, tr_sem, ps_sem, pr_sem, gs_sem, gr_sem,
+    ms_sem, mr_sem, ns_sem, nr_sem, zs_sem, zr_sem, ys_sem, yr_sem, y2s_sem, y2r_sem, os_sem, or_sem, ss_sem, sr_sem, hs_sem, hr_sem,
 ):
     r = lax.axis_index("req")
     t = lax.axis_index("tp")
@@ -56,7 +56,7 @@
     sibling = (r + 1 - 2 * core, t)
 
     tp_size = 2 * RING
-    after, before = (r, lax.rem(t + 1, tp_size)), (r, lax.rem(t + tp_size - 1, tp_size))
+    after = (r, lax.rem(t + 1, tp_size))
     y_next, y_prev = (lax.rem(r + 4, 16), t), (lax.rem(r + 12, 16), t)
 
     def column(k):
@@ -79,7 +79,7 @@
         return c
 
     barrier = pltpu.get_barrier_semaphore()
-    peers = [column(k) for k in range(1, RING)] + [inner, outer, sibling, after, before, y_next, y_prev]
+    peers = [(r, lax.rem(t + k, tp_size)) for k in range(1, tp_size)] + [outer, sibling, y_next, y_prev]
     for dev in peers:
         pl.semaphore_signal(barrier, inc=1, device_id=dev, device_id_type=MESH)
 
@@ -93,7 +93,7 @@
         c.start()
 
     wide = patch_ref[...].astype(jnp.float32)
-    xg[0] = layer_norm(wide, vg_ref[...]).astype(jnp.bfloat16)
+    xg[0] = layer_norm(wide, gain_ref[0:1]).astype(jnp.bfloat16)
     pl.semaphore_wait(barrier, len(peers))
 
     ag = {}
@@ -102,7 +102,6 @@
 
     n1 = w1_hbm.shape[0] // 4
     n2 = w2_hbm.shape[0] // 4
-    nm = wm_hbm.shape[0] // 2
     wx = []
     for i, dev in ((0, inner), (1, outer)):
         q = core * 2 + i
@@ -110,19 +109,23 @@
         a2 = pl.ds(pl.multiple_of(q * n2, 16), n2)
         wx.append((send(w1_hbm.at[a1], w1.at[1, a1], ws_sem.at[2 * i], wr_sem.at[2 * i], dev), w1.at[1, a1]))
         wx.append((send(w2_hbm.at[a2], w2.at[1, a2], ws_sem.at[2 * i + 1], wr_sem.at[2 * i + 1], dev), w2.at[1, a2]))
-    am = pl.ds(pl.multiple_of(core * nm, 16), nm)
-    wx.append((send(wm_hbm.at[am], wm.at[xl, am], ws_sem.at[4], wr_sem.at[4], inner), wm.at[1 - xl, am]))
-
     quarter = wc_hbm.shape[0] // 4
     y = r // 4
     s_w = 1 - 2 * core
     ahead = column(s_w)
 
     def quarter_at(k):
-        return pl.ds(pl.multiple_of(lax.rem(y + k, 4) * quarter, 8), quarter)
+        return pl.ds(pl.multiple_of(lax.rem(y + k, 4) * quarter, 16), quarter)
 
     def shard_at(k):
         return xl * RING + lax.rem(z - s_w * (k + 1) + RING, RING)
+
+    mx = []
+
+    def merge_weights():
+        for i, dev in ((0, inner), (1, outer)):
+            at = pl.ds(pl.multiple_of(core * 208 + 112 * i, 16), (112, 96)[i])
+            mx.append((send(wm_hbm.at[at], wm.at[xl, at], ms_sem.at[i], mr_sem.at[i], dev), wm.at[1 - xl, at]))
 
     zc = [send(wc_hbm.at[quarter_at(0)], wg.at[t, quarter_at(0)], zs_sem.at[0], zr_sem.at[0], ahead)]
     yc, y2c, xc, sc, hc = {}, {}, {}, [], []
@@ -173,7 +176,7 @@
 
     def window(k):
         if k == 0:
-            hc.append(send(ti, win.at[1], hs_sem.at[0], hr_sem.at[0], after))
+            hc.append(send(win.at[0], win.at[1], hs_sem.at[0], hr_sem.at[0], after))
             return
         hc[k - 1].wait_recv()
         if k < 4:
@@ -204,16 +207,16 @@
             from_y(step - 1)
         if step >= 2:
             to_x(step - 2)
-    ti[...] = rms_norm(text_ref[...].astype(jnp.float32), dg_ref[...]).astype(jnp.bfloat16)
-    own_window = pltpu.make_async_copy(ti, win.at[0], local_sem.at[4])
-    own_window.start()
+        if step == 1:
+            win[0] = rms_norm(text_ref[...].astype(jnp.float32), gain_ref[2:3]).astype(jnp.bfloat16)
     window(0)
 
     fwd = []
     for i, (c, ref) in enumerate(wx):
         c.wait_recv()
         fwd.append(send(ref, ref, fs_sem.at[i], fr_sem.at[i], sibling))
-    for c in fwd[:4]:
+    merge_weights()
+    for c in fwd:
         c.wait_recv()
 
     rs = {}
@@ -241,15 +244,19 @@
             to_x(2)
         if step == 1:
             to_x(3)
-            from_x(0)
+            mf = []
+            for i, (c, ref) in enumerate(mx):
+                c.wait_recv()
+                mf.append(send(ref, ref, ns_sem.at[i], nr_sem.at[i], sibling))
         if step == 2:
             window(1)
+            from_x(0)
         if step == 3:
             from_x(1)
     rs[0, 3].wait_recv()
     rs[1, 3].wait_recv()
-    total = acc[0] + rs_in[0, 3].astype(jnp.float32) + rs_in[1, 3].astype(jnp.float32)
-    nrm = layer_norm(patch_ref[...].astype(jnp.float32) + total, mg_ref[...]).astype(jnp.bfloat16)
+    summed = acc[0] + rs_in[0, 3].astype(jnp.float32) + rs_in[1, 3].astype(jnp.float32)
+    nrm = layer_norm(patch_ref[...].astype(jnp.float32) + summed, gain_ref[1:2]).astype(jnp.bfloat16)
 
     mrows = rows // 4
     width = wm_hbm.shape[0]
@@ -269,7 +276,8 @@
     frx[0] = fsend[z]
     window(2)
     loads[3].wait()
-    fwd[4].wait_recv()
+    for c in mf:
+        c.wait_recv()
     for c in a2a:
         c.wait_recv()
 
@@ -280,35 +288,83 @@
     for k in range(1, RING):
         red.append(send(psend.at[k], prx.at[RING - k], ps_sem.at[k], pr_sem.at[k], column(k)))
     from_x(2)
-    total = part[:mrows]
+    summed = part[:mrows]
     for c in red:
         c.wait_recv()
     for k in range(1, RING):
-        total = total + prx[k].astype(jnp.float32)
-    mg[t] = total.astype(jnp.bfloat16)
-
-    gat, xfw = [], [send(mg.at[t], mg.at[t], xs_sem.at[0], xr_sem.at[0], inner)]
-    for k in range(1, RING):
-        gat.append(send(mg.at[t], mg.at[t], gs_sem.at[k], gr_sem.at[k], column(k)))
+        summed = summed + prx[k].astype(jnp.float32)
+    mine[...] = summed.astype(jnp.bfloat16)
+
+    quad, lane4 = t // 4, lax.rem(t, 4)
+    gat = []
+    for i in range(2):
+        for k in range(4):
+            dest = lax.rem(quad + 2 + i, 4) * 4 + lax.rem(lane4 + k, 4)
+            gat.append(send(mine, mg.at[4 * i + lane4], gs_sem.at[4 * i + k], gr_sem.at[4 * i + k], (r, dest)))
     window(3)
     from_x(3)
-    for k in range(1, RING):
-        src = xl * RING + lax.rem(z - k + RING, RING)
-        gat[k - 1].wait_recv()
-        xfw.append(send(mg.at[src], mg.at[src], xs_sem.at[k], xr_sem.at[k], inner))
-    for c in xfw:
-        c.wait_recv()
-    out_ref[...] = mg[...].reshape(out_ref.shape)
+
+    seq = text_ref.shape[0]
+    depth = wc_hbm.shape[0] // 2
+    lane = lax.broadcasted_iota(jnp.int32, (1, 5 * seq), 1)
+    back = sum([(lane >= m * seq).astype(jnp.int32) for m in range(1, 5)])
+    kpos = (t - 2 * back) * seq + lane
+    qpos = t * seq + lax.broadcasted_iota(jnp.int32, (seq, 1), 0)
+    allowed = (kpos <= qpos) & (drow_ref[...] == dcol_ref[...])
+    bias[...] = jnp.where(allowed, 0.0, -1e30)
     window(4)
-    own_window.wait()
     for c in sc:
         c.wait_recv()
+    for c in hc:
+        c.wait_send()
+    for c in gat:
+        c.wait_recv()
+    raw = mg[...].reshape(8 * mrows, mg.shape[2])
+    image = rms_norm(raw.astype(jnp.float32), gain_ref[2:3]).astype(jnp.bfloat16)
+    for k in range(5):
+        pos = (t - k) * seq + lax.broadcasted_iota(jnp.int32, (seq, 1), 0)
+        onehot = (pos == slot_ref[...]).astype(jnp.float32)
+        hit = jnp.max(onehot, axis=1, keepdims=True) > 0.0
+        onehot = onehot.astype(jnp.bfloat16)
+        placed = jnp.dot(onehot, image, preferred_element_type=jnp.float32)
+        win[k] = jnp.where(hit, placed, win[k].astype(jnp.float32)).astype(jnp.bfloat16)
+        if k == 0:
+            placed = jnp.dot(onehot, raw, preferred_element_type=jnp.float32)
+            total[...] = jnp.where(hit, placed, text_ref[...].astype(jnp.float32))
+
+    lane = lax.broadcasted_iota(jnp.int32, (seq, depth), 1)
+    split = depth // 2
+
+    def head(h):
+        first, second = wg.at[h, :depth], wg.at[h, depth:]
+        x = win[...].reshape(5 * seq, win.shape[2])
+        kv = lax.dot_general(x, first[...], NT, preferred_element_type=jnp.float32).astype(jnp.bfloat16)
+        q = lax.dot_general(win[0], second[...], NT, preferred_element_type=jnp.float32)
+        q = jnp.where(lane < split, q, 0.0).astype(jnp.bfloat16)
+        scores = lax.dot_general(q, kv, NT, preferred_element_type=jnp.float32) * (1.0 / math.sqrt(HD)) + bias[...]
+        raised = jnp.exp(scores - jnp.max(scores, axis=1, keepdims=True))
+        mass = jnp.sum(raised, axis=1, keepdims=True)
+        mixed = jnp.dot(raised.astype(jnp.bfloat16), kv, preferred_element_type=jnp.float32) / mass
+        mixed = jnp.where(lane < split, 0.0, mixed).astype(jnp.bfloat16)
+        return jnp.dot(mixed, second[...], preferred_element_type=jnp.float32)
+
+    def two_heads(i, carry):
+        total[...] += head(2 * i) + head(2 * i + 1)
+        return carry
+
+    lax.fori_loop(0, wg.shape[0] // 2, two_heads, 0)
+    out_ref[...] = total[...].astype(jnp.bfloat16)
     for c in pending:
-        c.wait_send()
-
-
-def vision(patches, vg, mgain, text, dgain, w1, w2, wm, wc):
+        if not any(c is d for d in hc):
+            c.wait_send()
+
+
+NT = (((1,), (1,)), ((), ()))
+
+
+def block(patches, text, gains, slots, dcol, drow, w1, w2, wm, wc):
     rows, width = patches.shape
+    seq = text.shape[0]
     hidden = w1.shape[1]
     mrows = rows // 4
     bf, f32 = jnp.bfloat16, jnp.float32
@@ -317,15 +373,14 @@
     hbm = pl.BlockSpec(memory_space=pl.ANY)
     return pl.pallas_call(
         vision_kernel,
-        out_shape=(
-            jax.ShapeDtypeStruct((16 * mrows, width), bf),
-            jax.ShapeDtypeStruct((5, text.shape[0], width), bf),
-            jax.ShapeDtypeStruct((16, wc.shape[0], width), bf),
-        ),
-        in_specs=[vmem] * 5 + [hbm] * 4,
-        out_specs=(vmem, hbm, hbm),
+        out_shape=jax.ShapeDtypeStruct((seq, width), bf),
+        in_specs=[vmem] * 6 + [hbm] * 4,
+        out_specs=vmem,
         scratch_shapes=[
-            pltpu.VMEM(text.shape, bf),
+            pltpu.VMEM((5, seq, width), bf),
+            pltpu.VMEM((16, wc.shape[0], width), bf),
+            pltpu.VMEM((seq, 5 * seq), f32),
+            pltpu.VMEM((seq, width), f32),
             pltpu.VMEM((8, rows, width), bf),
             pltpu.VMEM((8, rows, width), f32),
             pltpu.VMEM((2, width, hidden), bf),
@@ -337,104 +392,44 @@
             pltpu.VMEM((8, 2, mrows, wm.shape[0]), bf),
             pltpu.VMEM((8, mrows, width), bf),
             pltpu.VMEM((8, mrows, width), bf),
-            pltpu.VMEM((16, mrows, width), bf),
-            dma((5,)), dma((5,)), dma((5,)), dma((5,)), dma((5,)),
+            pltpu.VMEM((8, mrows, width), bf),
+            pltpu.VMEM((mrows, width), bf),
+            dma((4,)), dma((4,)), dma((4,)), dma((4,)), dma((4,)),
             dma((2, 4)), dma((2, 4)), dma((2, 4)), dma((2, 4)),
-            dma((8,)), dma((8,)), dma((8,)), dma((8,)), dma((8,)), dma((8,)), dma((8,)), dma((8,)),
+            dma((8,)), dma((8,)), dma((8,)), dma((8,)), dma((8,)), dma((8,)),
+            dma((2,)), dma((2,)), dma((2,)), dma((2,)),
             dma((4,)), dma((4,)), dma((4, 2)), dma((4, 2)), dma((4,)), dma((4,)),
             dma((4, 2)), dma((4, 2)), dma((7,)), dma((7,)), dma((4,)), dma((4,)),
         ],
         compiler_params=pltpu.CompilerParams(
-            collective_id=0, has_side_effects=True, vmem_limit_bytes=56 * 2**20
+            collective_id=0, has_side_effects=True, vmem_limit_bytes=62 * 2**20
         ),
-        cost_estimate=pl.CostEstimate(flops=100_000_000_000, bytes_accessed=50_000_000, transcendentals=0),
-        name="vision",
-    )(patches, vg, mgain, text, dgain, w1, w2, wm, wc)
-
-
-NT = (((1,), (1,)), ((), ()))
-
-
-def decode_kernel(
-    win_ref, merged_ref, text_ref, gain_ref, slot_ref, kcol_ref, krow_ref, dcol_ref, drow_ref, w_ref, out_ref,
-    x, acc, bias,
-):
-    bf, f32 = jnp.bfloat16, jnp.float32
-    rows = text_ref.shape[0]
-    block = w_ref.shape[0] // 2
-
-    @pl.when(pl.program_id(0) == 0)
-    def _():
-        match = kcol_ref[...] == slot_ref[...]
-        onehot = match.astype(f32)
-        hit = jnp.max(onehot, axis=1, keepdims=True) > 0.0
-        onehot = onehot.astype(bf)
-        image = rms_norm(merged_ref[...].astype(f32), gain_ref[...]).astype(bf)
-        placed = jnp.dot(onehot, image, preferred_element_type=f32)
-        x[...] = jnp.where(hit, placed, win_ref[...].astype(f32)).astype(bf)
-        placed = jnp.dot(onehot[:rows], merged_ref[...], preferred_element_type=f32)
-        acc[...] = jnp.where(hit[:rows], placed, text_ref[...].astype(f32))
-        allowed = (krow_ref[...] <= kcol_ref[:rows, :]) & (drow_ref[...] == dcol_ref[...])
-        bias[...] = jnp.where(allowed, 0.0, -1e30)
-
-    lane = lax.broadcasted_iota(jnp.int32, (rows, block), 1)
-    kv = lax.dot_general(x[...], w_ref[:block], NT, preferred_element_type=f32).astype(bf)
-    q = lax.dot_general(x[:rows], w_ref[block:], NT, preferred_element_type=f32)
-    q = jnp.where(lane < HD, q, 0.0).astype(bf)
-    scores = lax.dot_general(q, kv, NT, preferred_element_type=f32) * (1.0 / math.sqrt(HD)) + bias[...]
-    raised = jnp.exp(scores - jnp.max(scores, axis=1, keepdims=True))
-    total = jnp.sum(raised, axis=1, keepdims=True)
-    mixed = jnp.dot(raised.astype(bf), kv, preferred_element_type=f32) / total
-    mixed = jnp.where(lane < HD, 0.0, mixed).astype(bf)
-    acc[...] += jnp.dot(mixed, w_ref[block:], preferred_element_type=f32)
-
-    @pl.when(pl.program_id(0) == pl.num_programs(0) - 1)
-    def _():
-        out_ref[...] = acc[...].astype(bf)
-
-
-def decode(win, merged, text, gain, slots, kcol, krow, dcol, drow, wg):
-    heads, depth, width = wg.shape
-    rows = text.shape[0]
-    span = win.shape[0]
-
-    def whole(a):
-        return pl.BlockSpec(a.shape, lambda h: (0,) * a.ndim)
-
-    args = (win, merged, text, gain, slots, kcol, krow, dcol, drow)
-    return pl.pallas_call(
-        decode_kernel,
-        grid=(heads,),
-        out_shape=jax.ShapeDtypeStruct((rows, width), jnp.bfloat16),
-        in_specs=[whole(a) for a in args] + [pl.BlockSpec((None, depth, width), lambda h: (h, 0, 0))],
-        out_specs=pl.BlockSpec((rows, width), lambda h: (0, 0)),
-        scratch_shapes=[
-            pltpu.VMEM((span, width), jnp.bfloat16),
-            pltpu.VMEM((rows, width), jnp.float32),
-            pltpu.VMEM((rows, span), jnp.float32),
-        ],
-        compiler_params=pltpu.CompilerParams(vmem_limit_bytes=50 * 2**20),
-        name="decode",
-    )(*args, wg)
+        name="block",
+    )(patches, text, gains, slots, dcol, drow, w1, w2, wm, wc)
 
 
 def shards(
     patches, vis_gain, w_fc1, w_fc2, merge_gain, w_merge, slots, text, docs, dec_gain, w_qkv, w_out
 ):
     text_rows = text[0]
-    rows = text_rows.shape[0]
+    rows, width = text_rows.shape
     across = w_qkv.T
-    wc = jnp.concatenate([across[HD:], across[:HD], w_out], axis=0)
-    merged, win, wg = vision(
-        patches[0], vis_gain[None], merge_gain[None], text_rows, dec_gain[None], w_fc1, w_fc2, w_merge, wc
+    gap = jnp.zeros((8, width), across.dtype)
+    wc = jnp.concatenate(
+        [across[HD:2 * HD], gap, across[2 * HD:], gap, across[:HD], gap, w_out, gap], axis=0
     )
+    gains = jnp.stack([vis_gain, merge_gain, dec_gain])
     t = lax.axis_index("tp")
     doc_pad = jnp.concatenate([jnp.full((4 * rows,), -1, jnp.int32), docs[0]])
     doc_win = lax.dynamic_slice_in_dim(doc_pad, t * rows, 5 * rows, 0).reshape(5, rows)[::-1].reshape(-1)
-    pos = ((t - jnp.arange(5, dtype=jnp.int32))[:, None] * rows + jnp.arange(rows, dtype=jnp.int32)).reshape(-1)
-    out = decode(
-        win.reshape(5 * rows, -1), merged, text_rows, dec_gain[None], slots,
-        pos[:, None], pos[None], doc_win[:rows, None], doc_win[None], wg,
+    image_slots = slots[0].reshape(4, -1)
+    quad = t // 4
+    near = jnp.concatenate([
+        lax.dynamic_index_in_dim(image_slots, lax.rem(quad + 2, 4), 0),
+        lax.dynamic_index_in_dim(image_slots, lax.rem(quad + 1, 4), 0),
+    ], axis=1)
+    out = block(
+        patches[0], text_rows, gains, near, doc_win[:rows, None], doc_win[None], w_fc1, w_fc2, w_merge, wc
     )
     return out[None]
 

time: 232 us -> 244 us (1.052)
  the two profiles are of different devices: /device:TPU:1 before, /device:TPU:12 now
where the time goes in v3:
time: 244 us; the launch traced here: 243 us
  Pallas kernels  232 us (95%)
  local copies, waits for them, and re-layouts  8.36 us (3%)
  other arithmetic  2.74 us (1%)
    pallas_call x1, Pallas kernels, block(): pl.pallas_call(vision_kernel, out_shape=jax.ShapeDtypeStruct((seq, width)...  232 us
    unnamed x19, local copies, waits for them, and re-layouts  5.92 us

profile of v3, /device:TPU:12, one launch (start us, length us, event | category | flops | bytes accessed | tf_op | source)
XLA Modules:
  0.0 243.3 jit_solution(9363587283351181092)
XLA Ops:
  0.0 0.0 copy-start.1
  0.0 0.5 broadcast.8
  0.5 1.3 reduce.3
  1.9 0.1 reshape_squeeze.3
  1.9 0.7 pad_add_fusion.slot_ref
  2.6 0.8 pad_dynamic-slice_fusion
  3.4 0.0 copy-start.2
  3.4 0.8 copy.13.dcol_ref
  4.2 0.0 copy-start.3
  4.2 0.0 copy-start.4
  4.2 0.1 reshape.8
  4.3 0.7 broadcast_in_dim_reshape.3.drow_ref
  4.9 1.0 slice_dynamic-update-slice_fusion.2
  6.0 1.0 slice_dynamic-update-slice_fusion.1
  7.0 1.0 slice_dynamic-update-slice_fusion
  8.0 0.0 copy-done.1
  8.1 0.0 copy-done.2
  8.1 0.0 copy-start
  8.1 0.0 copy-done.3
  8.1 0.0 copy-done.4
  8.2 0.7 pad_maximum_fusion.gain_ref
  8.9 0.3 copy-done
  9.2 232.1 %block.1 = bf16[192,1664]{1,0:T(8,128)(2,1)} custom-call(bf16[64,1664]{1,0:T(8,128)(2,1)} %bitcast.11, bf16[192,1664]{1,0:T(8,128)(2,1)} %bitcast.10, f32[3,1664]{1,0:T(4,128)} %pad_maximum_fusion.gain_ref, s32[1,128]{1,0:T(1,128)} %pad_add_fusion.slot_ref, s32[192,1]{1,0:T(8,128)} %copy.13.dcol_ref, s32[1,960]{1,0:T(1,128)} %broadcast_in_dim_reshape.3.drow_ref, ...), custom_call_target="tpu_custom_call" | custom-call | tf_op jit(solution)/shard_map/block/pallas_call | solution.py:374
  241.3 2.0 copy.22
  (11 shorter events, 0.1 us)
Async XLA Ops:
  0.0 8.0 %copy-start.1 = (bf16[104,1664]{1,0:T(8,128)(2,1)S(1)}, bf16[104,1664]{1,0:T(8,128)(2,1)}, u32[]{:S(2)}) copy-start(bf16[104,1664]{1,0:T(8,128)(2,1)} %param.23) | copy-start | bytes 1038340
  3.4 4.7 %copy-start.2 = (f32[1664]{0:T(1024)S(1)}, f32[1664]{0:T(1024)}, u32[]{:S(2)}) copy-start(f32[1664]{0:T(1024)} %param.13) | copy-start | bytes 19972
  4.2 4.0 %copy-start.3 = (f32[1664]{0:T(1024)S(1)}, f32[1664]{0:T(1024)}, u32[]{:S(2)}) copy-start(f32[1664]{0:T(1024)} %param.16) | copy-start | bytes 19972
  4.2 4.0 %copy-start.4 = (f32[1664]{0:T(1024)S(1)}, f32[1664]{0:T(1024)}, u32[]{:S(2)}) copy-start(f32[1664]{0:T(1024)} %param.21) | copy-start | bytes 19972
  8.1 1.1 copy-start

commit v4 on v3

--- a/solution.py
+++ b/solution.py
@@ -10,6 +10,10 @@
 
 HD = 104
 EPSILON = 1e-06
+PLAN = {
+    "A3": "z-1 h0", "R0": "z0", "R1": "z1", "R2": "z2 y0", "R3": "z3 h1", "L": "y1 x0", "T": "y2 x1 h2",
+    "M": "y3 x2 h3", "G": "x3 h4", "D0": "f0 h5", "D1": "f1", "D2": "f2", "D3": "f3",
+}
 MESH = pl.DeviceIdType.MESH
 RING = 8
 
@@ -38,9 +42,9 @@
 
 
 def vision_kernel(
-    patch_ref, text_ref, gain_ref, slot_ref, dcol_ref, drow_ref, w1_hbm, w2_hbm, wm_hbm, wc_hbm,
+    patch_ref, text_ref, vg_ref, mg_ref, dg_ref, slot_ref, doc_ref, wq_ref, wo_ref, w1_hbm, w2_hbm, wm_hbm,
     out_ref,
-    win, wg, bias, total, xg, acc, w1, w2, wm, rs_out, rs_in, fsend, frx, psend, prx, mg, mine,
+    win, relay, doc, wg, bias, total, xg, acc, w1, w2, wm, rs_out, rs_in, fsend, frx, psend, prx, mg, mine,
     local_sem, ws_sem, wr_sem, fs_sem, fr_sem, as_sem, ar_sem, rs_sem, rr_sem,
     ts_sem, tr_sem, ps_sem, pr_sem, gs_sem, gr_sem,
     ms_sem, mr_sem, ns_sem, nr_sem, zs_sem, zr_sem, ys_sem, yr_sem, y2s_sem, y2r_sem, os_sem, or_sem, ss_sem, sr_sem, hs_sem, hr_sem,
@@ -78,13 +82,13 @@
         pending.append(c)
         return c
 
+    mg[...] = jnp.zeros_like(mg)
     barrier = pltpu.get_barrier_semaphore()
     peers = [(r, lax.rem(t + k, tp_size)) for k in range(1, tp_size)] + [outer, sibling, y_next, y_prev]
     for dev in peers:
         pl.semaphore_signal(barrier, inc=1, device_id=dev, device_id_type=MESH)
 
     loads = [
-        pltpu.make_async_copy(wc_hbm, wg.at[t], local_sem.at[3]),
         pltpu.make_async_copy(w1_hbm, w1.at[0], local_sem.at[0]),
         pltpu.make_async_copy(w2_hbm, w2.at[0], local_sem.at[1]),
         pltpu.make_async_copy(wm_hbm, wm.at[xl], local_sem.at[2]),
@@ -93,7 +97,7 @@
         c.start()
 
     wide = patch_ref[...].astype(jnp.float32)
-    xg[0] = layer_norm(wide, gain_ref[0:1]).astype(jnp.bfloat16)
+    xg[0] = layer_norm(wide, vg_ref[...].reshape(1, -1)).astype(jnp.bfloat16)
     pl.semaphore_wait(barrier, len(peers))
 
     ag = {}
@@ -109,7 +113,7 @@
         a2 = pl.ds(pl.multiple_of(q * n2, 16), n2)
         wx.append((send(w1_hbm.at[a1], w1.at[1, a1], ws_sem.at[2 * i], wr_sem.at[2 * i], dev), w1.at[1, a1]))
         wx.append((send(w2_hbm.at[a2], w2.at[1, a2], ws_sem.at[2 * i + 1], wr_sem.at[2 * i + 1], dev), w2.at[1, a2]))
-    quarter = wc_hbm.shape[0] // 4
+    quarter = wg.shape[1] // 4
     y = r // 4
     s_w = 1 - 2 * core
     ahead = column(s_w)
@@ -127,10 +131,26 @@
             at = pl.ds(pl.multiple_of(core * 208 + 112 * i, 16), (112, 96)[i])
             mx.append((send(wm_hbm.at[at], wm.at[xl, at], ms_sem.at[i], mr_sem.at[i], dev), wm.at[1 - xl, at]))
 
-    zc = [send(wc_hbm.at[quarter_at(0)], wg.at[t, quarter_at(0)], zs_sem.at[0], zr_sem.at[0], ahead)]
+    row = lax.broadcasted_iota(jnp.int32, (3 * quarter, 3 * HD), 0)
+    col = lax.broadcasted_iota(jnp.int32, (3 * quarter, 3 * HD), 1)
+    second = (row >= quarter).astype(jnp.int32)
+    third = (row >= 2 * quarter).astype(jnp.int32)
+    inside = row - quarter * (second + third)
+    pick = (col == inside + HD * (1 + second - 2 * third)) & (inside < HD)
+    pick = pick.astype(jnp.float32).astype(jnp.bfloat16)
+    wg[t, :3 * quarter] = jnp.dot(pick, wq_ref[...], preferred_element_type=jnp.float32).astype(jnp.bfloat16)
+    row = lax.broadcasted_iota(jnp.int32, (quarter, HD), 0)
+    col = lax.broadcasted_iota(jnp.int32, (quarter, HD), 1)
+    pick = (row == col).astype(jnp.float32).astype(jnp.bfloat16)
+    wg[t, 3 * quarter:] = jnp.dot(pick, wo_ref[...], preferred_element_type=jnp.float32).astype(jnp.bfloat16)
+
+    zc = []
     yc, y2c, xc, sc, hc = {}, {}, {}, [], []
 
     def from_column(k):
+        if k < 0:
+            zc.append(send(wg.at[t, quarter_at(0)], wg.at[t, quarter_at(0)], zs_sem.at[0], zr_sem.at[0], ahead))
+            return
         piece = wg.at[shard_at(k), quarter_at(0)]
         zc[k].wait_recv()
         if k < 3:
@@ -147,13 +167,12 @@
         y2c[k] = send(piece, piece, y2s_sem.at[k], y2r_sem.at[k], y_next if k % 2 == 0 else y_prev)
 
     def both_halves(ref, i):
-        n = wc_hbm.shape[0] // 2
+        n = wg.shape[1] // 2
         return ref.at[pl.ds(i * n, n)]
 
     def to_x(k):
         y2c[k].wait_recv()
         if k == 3:
-            loads[0].wait()
             idx = xl * RING + lax.rem(z + 4 - 4 * core, RING)
         else:
             idx = shard_at(k)
@@ -174,13 +193,33 @@
             c.wait_recv()
         sc.append(send(wg.at[idx], wg.at[idx], ss_sem.at[3 + k], sr_sem.at[3 + k], sibling))
 
+    cut = 128
+    keep = slice(0, cut)
+    rest = slice(cut, text_ref.shape[0])
+    back = (r, lax.rem(t + tp_size - 1, tp_size))
+    across = (r, lax.rem(xl * RING + lax.rem(z + 3, RING) + 4, tp_size))
+
     def window(k):
+        if k > 0:
+            for c in hc[-2:] if k < 5 else hc[-1:]:
+                c.wait_recv()
+        if k < 4:
+            hc.append(send(win.at[k, keep], win.at[k + 1, keep], hs_sem.at[k], hr_sem.at[k], after))
         if k == 0:
-            hc.append(send(win.at[0], win.at[1], hs_sem.at[0], hr_sem.at[0], after))
-            return
-        hc[k - 1].wait_recv()
-        if k < 4:
-            hc.append(send(win.at[k], win.at[k + 1], hs_sem.at[k], hr_sem.at[k], after))
+            src, dst, dev = win.at[0, rest], relay, column(-3)
+        elif k == 1:
+            src, dst, dev = relay, win.at[4, rest], across
+        elif k < 5:
+            src, dst, dev = win.at[6 - k, rest], win.at[5 - k, rest], back
+        if k < 5:
+            hc.append(send(src, dst, hs_sem.at[4 + k], hr_sem.at[4 + k], dev))
+
+    def serve(point):
+        for name in PLAN.get(point, "").split():
+            act = {"z": from_column, "y": from_y, "x": to_x, "f": from_x, "h": window}[name[0]]
+            act(int(name[1:]))
+
+    serve("S")
 
     def mlp(pair, which):
         x = xg[2 * pair:2 * pair + 2].reshape(2 * rows, xg.shape[2])
@@ -198,18 +237,13 @@
                     src, dst = src.at[part], dst.at[part]
                 ag[d, step + 1] = send(src, dst, as_sem.at[d, step + 1], ar_sem.at[d, step + 1], column(s))
         if step == 0:
+            loads[0].wait()
             loads[1].wait()
-            loads[2].wait()
         pair = (step + 1) % 4
         acc[2 * pair:2 * pair + 2] = mlp(pair, 0)
-        from_column(step)
-        if step >= 1:
-            from_y(step - 1)
-        if step >= 2:
-            to_x(step - 2)
-        if step == 1:
-            win[0] = rms_norm(text_ref[...].astype(jnp.float32), gain_ref[2:3]).astype(jnp.bfloat16)
-    window(0)
+        if step == 0:
+            win[0] = rms_norm(text_ref[...].astype(jnp.float32), dg_ref[...].reshape(1, -1)).astype(jnp.bfloat16)
+        serve("A%d" % step)
 
     fwd = []
     for i, (c, ref) in enumerate(wx):
@@ -239,25 +273,18 @@
             else:
                 out[...] = (block[...] + rs_in[d, step - 1].astype(jnp.float32)).astype(jnp.bfloat16)
             rs[d, step] = send(out, rs_in.at[d, step], rs_sem.at[d, step], rr_sem.at[d, step], column(s))
-        if step == 0:
-            from_y(3)
-            to_x(2)
         if step == 1:
-            to_x(3)
             mf = []
             for i, (c, ref) in enumerate(mx):
                 c.wait_recv()
                 mf.append(send(ref, ref, ns_sem.at[i], nr_sem.at[i], sibling))
-        if step == 2:
-            window(1)
-            from_x(0)
-        if step == 3:
-            from_x(1)
+        serve("R%d" % step)
     rs[0, 3].wait_recv()
     rs[1, 3].wait_recv()
     summed = acc[0] + rs_in[0, 3].astype(jnp.float32) + rs_in[1, 3].astype(jnp.float32)
-    nrm = layer_norm(patch_ref[...].astype(jnp.float32) + summed, gain_ref[1:2]).astype(jnp.bfloat16)
-
+    nrm = layer_norm(patch_ref[...].astype(jnp.float32) + summed, mg_ref[...].reshape(1, -1)).astype(jnp.bfloat16)
+
+    serve("L")
     mrows = rows // 4
     width = wm_hbm.shape[0]
     to_row = lax.broadcasted_iota(jnp.int32, (rows, rows), 0)
@@ -274,8 +301,8 @@
         dest = lax.rem(z + k, RING)
         a2a.append(send(fsend.at[dest], frx.at[RING - k], ts_sem.at[k], tr_sem.at[k], column(k)))
     frx[0] = fsend[z]
-    window(2)
-    loads[3].wait()
+    serve("T")
+    loads[2].wait()
     for c in mf:
         c.wait_recv()
     for c in a2a:
@@ -287,7 +314,7 @@
     red = []
     for k in range(1, RING):
         red.append(send(psend.at[k], prx.at[RING - k], ps_sem.at[k], pr_sem.at[k], column(k)))
-    from_x(2)
+    serve("M")
     summed = part[:mrows]
     for c in red:
         c.wait_recv()
@@ -300,27 +327,31 @@
     for i in range(2):
         for k in range(4):
             dest = lax.rem(quad + 2 + i, 4) * 4 + lax.rem(lane4 + k, 4)
-            gat.append(send(mine, mg.at[4 * i + lane4], gs_sem.at[4 * i + k], gr_sem.at[4 * i + k], (r, dest)))
-    window(3)
-    from_x(3)
+            gat.append(send(mine, mg.at[t], gs_sem.at[4 * i + k], gr_sem.at[4 * i + k], (r, dest)))
+    serve("G")
 
     seq = text_ref.shape[0]
-    depth = wc_hbm.shape[0] // 2
-    lane = lax.broadcasted_iota(jnp.int32, (1, 5 * seq), 1)
-    back = sum([(lane >= m * seq).astype(jnp.int32) for m in range(1, 5)])
-    kpos = (t - 2 * back) * seq + lane
-    qpos = t * seq + lax.broadcasted_iota(jnp.int32, (seq, 1), 0)
-    allowed = (kpos <= qpos) & (drow_ref[...] == dcol_ref[...])
-    bias[...] = jnp.where(allowed, 0.0, -1e30)
-    window(4)
-    for c in sc:
+    depth = wg.shape[1] // 2
+    row = lax.broadcasted_iota(jnp.int32, (seq, seq), 0)
+    col = lax.broadcasted_iota(jnp.int32, (seq, seq), 1)
+    for k in range(tp_size):
+        doc[k:k + 1] = doc_ref[:, k * seq:(k + 1) * seq].astype(jnp.float32)
+    own = doc[pl.ds(t, 1), :]
+    own = jnp.sum(jnp.where(row == col, own, 0.0), axis=1, keepdims=True)
+    for k in range(5):
+        theirs = doc[pl.ds(lax.rem(t - k + tp_size, tp_size), 1), :]
+        kpos = (t - k) * seq + col
+        allowed = (kpos >= 0) & (kpos <= t * seq + row) & (theirs == own)
+        bias[:, k * seq:(k + 1) * seq] = jnp.where(allowed, 0.0, -1e30)
+    serve("D0")
+    for c in sc[:3]:
         c.wait_recv()
     for c in hc:
         c.wait_send()
     for c in gat:
         c.wait_recv()
-    raw = mg[...].reshape(8 * mrows, mg.shape[2])
-    image = rms_norm(raw.astype(jnp.float32), gain_ref[2:3]).astype(jnp.bfloat16)
+    raw = mg[...].reshape(tp_size * mrows, mg.shape[2])
+    image = rms_norm(raw.astype(jnp.float32), dg_ref[...].reshape(1, -1)).astype(jnp.bfloat16)
     for k in range(5):
         pos = (t - k) * seq + lax.broadcasted_iota(jnp.int32, (seq, 1), 0)
         onehot = (pos == slot_ref[...]).astype(jnp.float32)
@@ -335,24 +366,44 @@
     lane = lax.broadcasted_iota(jnp.int32, (seq, depth), 1)
     split = depth // 2
 
-    def head(h):
-        first, second = wg.at[h, :depth], wg.at[h, depth:]
+    def decode(side, *pairs):
+        heads = []
+        for p in pairs:
+            heads.append(side * RING + lax.rem(z + p, RING))
+            heads.append(side * RING + lax.rem(z + RING - p + (4 if p == 0 else 0), RING))
         x = win[...].reshape(5 * seq, win.shape[2])
-        kv = lax.dot_general(x, first[...], NT, preferred_element_type=jnp.float32).astype(jnp.bfloat16)
-        q = lax.dot_general(win[0], second[...], NT, preferred_element_type=jnp.float32)
-        q = jnp.where(lane < split, q, 0.0).astype(jnp.bfloat16)
-        scores = lax.dot_general(q, kv, NT, preferred_element_type=jnp.float32) * (1.0 / math.sqrt(HD)) + bias[...]
-        raised = jnp.exp(scores - jnp.max(scores, axis=1, keepdims=True))
-        mass = jnp.sum(raised, axis=1, keepdims=True)
-        mixed = jnp.dot(raised.astype(jnp.bfloat16), kv, preferred_element_type=jnp.float32) / mass
-        mixed = jnp.where(lane < split, 0.0, mixed).astype(jnp.bfloat16)
-        return jnp.dot(mixed, second[...], preferred_element_type=jnp.float32)
-
-    def two_heads(i, carry):
-        total[...] += head(2 * i) + head(2 * i + 1)
-        return carry
-
-    lax.fori_loop(0, wg.shape[0] // 2, two_heads, 0)
+        first = win[0]
+        kvs = [
+            lax.dot_general(x, wg[h, :depth], NT, preferred_element_type=jnp.float32).astype(jnp.bfloat16)
+            for h in heads
+        ]
+        qs = [lax.dot_general(first, wg[h, depth:], NT, preferred_element_type=jnp.float32) for h in heads]
+        qs = [jnp.where(lane < split, q, 0.0).astype(jnp.bfloat16) for q in qs]
+        scores = [
+            lax.dot_general(q, kv, NT, preferred_element_type=jnp.float32) * (1.0 / math.sqrt(HD)) + bias[...]
+            for q, kv in zip(qs, kvs)
+        ]
+        raised = [jnp.exp(s - jnp.max(s, axis=1, keepdims=True)) for s in scores]
+        mass = [jnp.sum(e, axis=1, keepdims=True) for e in raised]
+        mixed = [
+            (jnp.dot(e.astype(jnp.bfloat16), kv, preferred_element_type=jnp.float32) / m)[:, split:]
+            for e, kv, m in zip(raised, kvs, mass)
+        ]
+        outs = jnp.concatenate([wg[h, depth + split:] for h in heads], axis=0)
+        mixed = jnp.concatenate(mixed, axis=1).astype(jnp.bfloat16)
+        total[...] += jnp.dot(mixed, outs, preferred_element_type=jnp.float32)
+
+    decode(xl, 0, 1)
+    serve("D1")
+    decode(xl, 2, 3)
+    serve("D2")
+    for c in sc[3:5]:
+        c.wait_recv()
+    decode(1 - xl, 1, 2)
+    serve("D3")
+    for c in sc[5:]:
+        c.wait_recv()
+    decode(1 - xl, 3, 0)
     out_ref[...] = total[...].astype(jnp.bfloat16)
     for c in pending:
         if not any(c is d for d in hc):
@@ -362,7 +413,7 @@
 NT = (((1,), (1,)), ((), ()))
 
 
-def block(patches, text, gains, slots, dcol, drow, w1, w2, wm, wc):
+def block(patches, text, vg, mgain, dgain, slots, docs, wq, wo, w1, w2, wm):
     rows, width = patches.shape
     seq = text.shape[0]
     hidden = w1.shape[1]
@@ -374,11 +425,13 @@
     return pl.pallas_call(
         vision_kernel,
         out_shape=jax.ShapeDtypeStruct((seq, width), bf),
-        in_specs=[vmem] * 6 + [hbm] * 4,
+        in_specs=[vmem] * 9 + [hbm] * 3,
         out_specs=vmem,
         scratch_shapes=[
             pltpu.VMEM((5, seq, width), bf),
-            pltpu.VMEM((16, wc.shape[0], width), bf),
+            pltpu.VMEM((seq - 128, width), bf),
+            pltpu.VMEM((16, seq), f32),
+            pltpu.VMEM((16, 4 * 112, width), bf),
             pltpu.VMEM((seq, 5 * seq), f32),
             pltpu.VMEM((seq, width), f32),
             pltpu.VMEM((8, rows, width), bf),
@@ -392,44 +445,29 @@
             pltpu.VMEM((8, 2, mrows, wm.shape[0]), bf),
             pltpu.VMEM((8, mrows, width), bf),
             pltpu.VMEM((8, mrows, width), bf),
-            pltpu.VMEM((8, mrows, width), bf),
+            pltpu.VMEM((16, mrows, width), bf),
             pltpu.VMEM((mrows, width), bf),
             dma((4,)), dma((4,)), dma((4,)), dma((4,)), dma((4,)),
             dma((2, 4)), dma((2, 4)), dma((2, 4)), dma((2, 4)),
             dma((8,)), dma((8,)), dma((8,)), dma((8,)), dma((8,)), dma((8,)),
             dma((2,)), dma((2,)), dma((2,)), dma((2,)),
             dma((4,)), dma((4,)), dma((4, 2)), dma((4, 2)), dma((4,)), dma((4,)),
-            dma((4, 2)), dma((4, 2)), dma((7,)), dma((7,)), dma((4,)), dma((4,)),
+            dma((4, 2)), dma((4, 2)), dma((7,)), dma((7,)), dma((9,)), dma((9,)),
         ],
         compiler_params=pltpu.CompilerParams(
             collective_id=0, has_side_effects=True, vmem_limit_bytes=62 * 2**20
         ),
         name="block",
-    )(patches, text, gains, slots, dcol, drow, w1, w2, wm, wc)
+    )(patches, text, vg, mgain, dgain, slots, docs, wq, wo, w1, w2, wm)
 
 
 def shards(
     patches, vis_gain, w_fc1, w_fc2, merge_gain, w_merge, slots, text, docs, dec_gain, w_qkv, w_out
 ):
     text_rows = text[0]
-    rows, width = text_rows.shape
-    across = w_qkv.T
-    gap = jnp.zeros((8, width), across.dtype)
-    wc = jnp.concatenate(
-        [across[HD:2 * HD], gap, across[2 * HD:], gap, across[:HD], gap, w_out, gap], axis=0
-    )
-    gains = jnp.stack([vis_gain, merge_gain, dec_gain])
-    t = lax.axis_index("tp")
-    doc_pad = jnp.concatenate([jnp.full((4 * rows,), -1, jnp.int32), docs[0]])
-    doc_win = lax.dynamic_slice_in_dim(doc_pad, t * rows, 5 * rows, 0).reshape(5, rows)[::-1].reshape(-1)
-    image_slots = slots[0].reshape(4, -1)
-    quad = t // 4
-    near = jnp.concatenate([
-        lax.dynamic_index_in_dim(image_slots, lax.rem(quad + 2, 4), 0),
-        lax.dynamic_index_in_dim(image_slots, lax.rem(quad + 1, 4), 0),
-    ], axis=1)
     out = block(
-        patches[0], text_rows, gains, near, doc_win[:rows, None], doc_win[None], w_fc1, w_fc2, w_merge, wc
+        patches[0], text_rows, vis_gain, merge_gain, dec_gain, slots, docs, w_qkv.T, w_out,
+        w_fc1, w_fc2, w_merge,
     )
     return out[None]
 

time: 244 us -> 195 us (0.80)
  the two profiles are of different devices: /device:TPU:12 before, /device:TPU:1 now
where the time goes in v4:
time: 195 us; the launch traced here: 193 us
  Pallas kernels  191 us (98%)
  local copies, waits for them, and re-layouts  1.96 us (1%)
    pallas_call x1, Pallas kernels, block(): pl.pallas_call(vision_kernel, out_shape=jax.ShapeDtypeStruct((seq, width)...  191 us

profile of v4, /device:TPU:1, one launch (start us, length us, event | category | flops | bytes accessed | tf_op | source)
XLA Modules:
  0.0 193.1 jit_solution(17065305888766896665)
XLA Ops:
  0.0 191.2 %block.1 = bf16[192,1664]{1,0:T(8,128)(2,1)} custom-call(bf16[64,1664]{1,0:T(8,128)(2,1)} %bitcast.7, bf16[192,1664]{1,0:T(8,128)(2,1)} %bitcast.6, f32[1664]{0:T(1024)} %vg_ref.1, f32[1664]{0:T(1024)} %mg_ref.1, f32[1664]{0:T(1024)} %dg_ref.1, s32[1,256]{1,0:T(1,128)} %slot_ref.1, s32[1,3072]{1,0:T(1,128)} %doc_ref.1, bf16[312,1664]{1,0:T(8,128)(2,1)} %bitcast.5, ...), custom_call_target="tpu_custom_call" | custom-call | tf_op jit(solution)/shard_map/block/pallas_call | solution.py:425
  191.2 2.0 %copy.14 = bf16[1,192,1664]{2,1,0:T(8,128)(2,1)} copy(bf16[1,192,1664]{2,1,0:T(8,128)(2,1)} %bitcast.4) | data formatting | bytes 1277952

commit v5 on v4

--- a/solution.py
+++ b/solution.py
@@ -11,8 +11,8 @@
 HD = 104
 EPSILON = 1e-06
 PLAN = {
-    "A3": "z-1 h0", "R0": "z0", "R1": "z1", "R2": "z2 y0", "R3": "z3 h1", "L": "y1 x0", "T": "y2 x1 h2",
-    "M": "y3 x2 h3", "G": "x3 h4", "D0": "f0 h5", "D1": "f1", "D2": "f2", "D3": "f3",
+    "A1": "z-1", "A2": "z0", "A3": "z1 h0", "R0": "z2 y0", "R1": "z3", "R2": "y1 x0", "R3": "y2 h1", "L": "x1",
+    "T": "y3 h2", "M": "x2 h3", "G": "x3 f0 h4", "D0": "h5", "D1": "f1", "D2": "f2", "D3": "f3",
 }
 MESH = pl.DeviceIdType.MESH
 RING = 8

time: 195 us -> 193 us (0.990)
  Pallas kernels: 191 us -> 189 us
where the time goes in v5:
time: 193 us; the launch traced here: 191 us
  Pallas kernels  189 us (98%)
  local copies, waits for them, and re-layouts  1.96 us (1%)
    pallas_call x1, Pallas kernels, block(): pl.pallas_call(vision_kernel, out_shape=jax.ShapeDtypeStruct((seq, width)...  189 us

profile of v5, /device:TPU:1, one launch (start us, length us, event | category | flops | bytes accessed | tf_op | source)
XLA Modules:
  0.0 191.3 jit_solution(3182421016458708478)
XLA Ops:
  0.0 189.3 %block.1 = bf16[192,1664]{1,0:T(8,128)(2,1)} custom-call(bf16[64,1664]{1,0:T(8,128)(2,1)} %bitcast.7, bf16[192,1664]{1,0:T(8,128)(2,1)} %bitcast.6, f32[1664]{0:T(1024)} %vg_ref.1, f32[1664]{0:T(1024)} %mg_ref.1, f32[1664]{0:T(1024)} %dg_ref.1, s32[1,256]{1,0:T(1,128)} %slot_ref.1, s32[1,3072]{1,0:T(1,128)} %doc_ref.1, bf16[312,1664]{1,0:T(8,128)(2,1)} %bitcast.5, ...), custom_call_target="tpu_custom_call" | custom-call | tf_op jit(solution)/shard_map/block/pallas_call | solution.py:425
  189.3 2.0 %copy.14 = bf16[1,192,1664]{2,1,0:T(8,128)(2,1)} copy(bf16[1,192,1664]{2,1,0:T(8,128)(2,1)} %bitcast.4) | data formatting | bytes 1277952

commit v6 on v5

--- a/solution.py
+++ b/solution.py
@@ -11,8 +11,8 @@
 HD = 104
 EPSILON = 1e-06
 PLAN = {
-    "A1": "z-1", "A2": "z0", "A3": "z1 h0", "R0": "z2 y0", "R1": "z3", "R2": "y1 x0", "R3": "y2 h1", "L": "x1",
-    "T": "y3 h2", "M": "x2 h3", "G": "x3 f0 h4", "D0": "h5", "D1": "f1", "D2": "f2", "D3": "f3",
+    "A0": "h0", "A3": "h1 z-1", "R0": "z0", "R1": "z1 h2", "R2": "z2 y0", "R3": "h3 z3", "L": "y1 x0",
+    "T": "h4 y2 x1", "M": "h5 y3 x2", "G": "x3", "D0": "f0", "D1": "f1", "D2": "f2", "D3": "f3",
 }
 MESH = pl.DeviceIdType.MESH
 RING = 8

time: 193 us -> 198 us (1.026)
  Pallas kernels: 189 us -> 194 us
    pallas_call x1, Pallas kernels: 189 us -> 194 us  [block(): pl.pallas_call(vision_kernel, out_shape=jax.ShapeDtypeStruct((seq, width)...]
where the time goes in v6:
time: 198 us; the launch traced here: 196 us
  Pallas kernels  194 us (98%)
    pallas_call x1, Pallas kernels, block(): pl.pallas_call(vision_kernel, out_shape=jax.ShapeDtypeStruct((seq, width)...  194 us

profile of v6, /device:TPU:1, one launch (start us, length us, event | category | flops | bytes accessed | tf_op | source)
XLA Modules:
  0.0 196.2 jit_solution(4725098824678302693)
XLA Ops:
  0.0 194.3 %block.1 = bf16[192,1664]{1,0:T(8,128)(2,1)} custom-call(bf16[64,1664]{1,0:T(8,128)(2,1)} %bitcast.7, bf16[192,1664]{1,0:T(8,128)(2,1)} %bitcast.6, f32[1664]{0:T(1024)} %vg_ref.1, f32[1664]{0:T(1024)} %mg_ref.1, f32[1664]{0:T(1024)} %dg_ref.1, s32[1,256]{1,0:T(1,128)} %slot_ref.1, s32[1,3072]{1,0:T(1,128)} %doc_ref.1, bf16[312,1664]{1,0:T(8,128)(2,1)} %bitcast.5, ...), custom_call_target="tpu_custom_call" | custom-call | tf_op jit(solution)/shard_map/block/pallas_call | solution.py:425
  194.3 2.0 copy.14

commit v7 on v6

--- a/solution.py
+++ b/solution.py
@@ -11,8 +11,8 @@
 HD = 104
 EPSILON = 1e-06
 PLAN = {
-    "A0": "h0", "A3": "h1 z-1", "R0": "z0", "R1": "z1 h2", "R2": "z2 y0", "R3": "h3 z3", "L": "y1 x0",
-    "T": "h4 y2 x1", "M": "h5 y3 x2", "G": "x3", "D0": "f0", "D1": "f1", "D2": "f2", "D3": "f3",
+    "A1": "z-1", "A2": "z0", "A3": "z1 h0", "R0": "z2 y0", "R1": "z3", "R2": "y1 x0 h1", "R3": "y2", "L": "x1 h2",
+    "T": "y3", "M": "x2 h3", "G": "x3 f0 h4", "D0": "h5", "D1": "f1", "D2": "f2", "D3": "f3",
 }
 MESH = pl.DeviceIdType.MESH
 RING = 8

time: 198 us -> 192 us (0.970)
  Pallas kernels: 194 us -> 190 us
    pallas_call x1, Pallas kernels: 194 us -> 190 us  [block(): pl.pallas_call(vision_kernel, out_shape=jax.ShapeDtypeStruct((seq, width)...]
where the time goes in v7:
time: 192 us
  Pallas kernels  190 us (99%)
  local copies, waits for them, and re-layouts  1.96 us (1%)
    pallas_call x1, Pallas kernels, block(): pl.pallas_call(vision_kernel, out_shape=jax.ShapeDtypeStruct((seq, width)...  190 us

profile of v7, /device:TPU:1, one launch (start us, length us, event | category | flops | bytes accessed | tf_op | source)
XLA Modules:
  0.0 191.6 jit_solution(17661013326239983683)
XLA Ops:
  0.0 189.6 %block.1 = bf16[192,1664]{1,0:T(8,128)(2,1)} custom-call(bf16[64,1664]{1,0:T(8,128)(2,1)} %bitcast.7, bf16[192,1664]{1,0:T(8,128)(2,1)} %bitcast.6, f32[1664]{0:T(1024)} %vg_ref.1, f32[1664]{0:T(1024)} %mg_ref.1, f32[1664]{0:T(1024)} %dg_ref.1, s32[1,256]{1,0:T(1,128)} %slot_ref.1, s32[1,3072]{1,0:T(1,128)} %doc_ref.1, bf16[312,1664]{1,0:T(8,128)(2,1)} %bitcast.5, ...), custom_call_target="tpu_custom_call" | custom-call | tf_op jit(solution)/shard_map/block/pallas_call | solution.py:425
  189.6 2.0 %copy.14 = bf16[1,192,1664]{2,1,0:T(8,128)(2,1)} copy(bf16[1,192,1664]{2,1,0:T(8,128)(2,1)} %bitcast.4) | data formatting | bytes 1277952
